TPU v7x, 32 devices: a whole 2x2x4 slice. The times are simulated.
32 devices in a mesh: dev: 32 (over z, y, x, core).
Axes of the slice: x: 2, y: 2, z: 4, core: 2. Of those that a mesh axis runs over, the one named last changes fastest.
Arguments:
- embeddings: bfloat16 [32768, 128], P('dev'), may hold values from -6 to 6
- ranks: int32 [32768], P('dev'), may hold values from 0 to 32767, as said below
- pair_weight: bfloat16 [256, 128], replicated, may hold values from -0.375 to 0.375
- pair_bias: float32 [128], replicated, may hold values from -3 to 3
- score_weight: bfloat16 [128], replicated, may hold values from -0.5 to 0.5
Outputs:
- scores: float32 [31, 32768], P(None, 'dev')
Inputs may be any that keep to these rules, and one draw needn't show every extreme that they name: ranks is a permutation of 0 .. 32767. Of the records of one device, at most 64 have ranks in any one range [o * 1024, (o + 1) * 1024); on every device some range holds exactly 64 of them, and every range holds exactly 64 of some device's records.
All inputs are finite; a program needn't handle non-finite values.
Results may differ from a plain program's by a relative error of at most 0.0045.
Values may be sent and summed in bfloat16 or wider, within the bound.
No kernel may reach another device: no remote copies, remote signals or barrier semaphores. Data moves between devices by JAX's collectives and lax.ppermute only.
A program may use at most 64 MiB of HBM per device.

v0:
```python
import jax
import jax.numpy as jnp
from jax import lax
from jax.sharding import PartitionSpec as P

WIN = 32


def from_behind(value, axis, steps):
    count = lax.axis_size(axis)
    initial, last = (max(0, -steps), min(count, count - steps))
    return lax.ppermute(value, axis, [(source, source + steps) for source in range(initial, last)])


def body(embeddings, ranks, pair_weight, pair_bias, score_weight):
    rows_dev = embeddings.shape[0]
    width = embeddings.shape[1]
    devices = lax.axis_size("dev")
    my_index = lax.axis_index("dev")
    margin = WIN - 1
    capacity = 2 * rows_dev // devices
    by_rank = jnp.argsort(ranks)
    ranked = ranks[by_rank]
    owners = ranked // rows_dev
    owner_ids = jnp.arange(devices, dtype=jnp.int32)
    member = owners[:, None] == owner_ids[None, :]
    counts = jnp.sum(member.astype(jnp.int32), axis=0)
    starts = jnp.cumsum(counts) - counts
    dropped = rows_dev + margin
    places = jnp.arange(capacity, dtype=jnp.int32)
    slot_index = jnp.clip(starts[:, None] + places[None, :], 0, rows_dev - 1)
    is_live = places[None, :] < counts[:, None]
    source_rows = by_rank[slot_index]
    target = jnp.where(is_live, ranked[slot_index] - owner_ids[:, None] * rows_dev, dropped)
    outgoing = embeddings[source_rows.reshape(-1)]
    arrived, positions = (
        lax.all_to_all(outgoing, "dev", split_axis=0, concat_axis=0, tiled=True),
        lax.all_to_all(target.reshape(-1), "dev", split_axis=0, concat_axis=0, tiled=True),
    )
    extended = (
        jnp.zeros((rows_dev + margin, width), jnp.bfloat16).at[positions].set(arrived, mode="drop")
    )
    local_rows = extended[:rows_dev]
    following = from_behind(local_rows[:margin], "dev", -1)
    extended = jnp.concatenate([local_rows, following], axis=0)
    leading = extended[:rows_dev].astype(jnp.float32)
    weight_product = pair_weight[:width]
    weight_distance = pair_weight[width:]

    def score_offset(offset):
        partner = lax.dynamic_slice_in_dim(extended, offset, rows_dev, 0).astype(jnp.float32)
        product = (leading * partner).astype(jnp.bfloat16)
        distance = jnp.abs(leading - partner).astype(jnp.bfloat16)
        hidden = jnp.dot(product, weight_product, preferred_element_type=jnp.float32)
        hidden = (
            hidden
            + jnp.dot(distance, weight_distance, preferred_element_type=jnp.float32)
            + pair_bias
        )
        hidden = jax.nn.relu(hidden).astype(jnp.bfloat16)
        return jnp.dot(hidden, score_weight, preferred_element_type=jnp.float32)

    offsets = jnp.arange(1, WIN, dtype=jnp.int32)
    scores = lax.map(score_offset, offsets)
    global_pos = my_index * rows_dev + jnp.arange(rows_dev, dtype=jnp.int32)
    inside = global_pos[None, :] + offsets[:, None] < devices * rows_dev
    return jnp.where(inside, scores, jnp.zeros_like(scores))


def solution(mesh):
    placed = (P("dev", None), P("dev"), P(), P(), P())
    return jax.shard_map(
        body, mesh=mesh, in_specs=placed, out_specs=P(None, "dev"), check_vma=False
    )
```

profile of v0, /device:TPU:1, one launch (start us, length us, event | category | flops | bytes accessed | tf_op | source)
XLA Modules:
  0.0 177.7 jit_solution(12008024207637797555)
XLA Ops:
  0.0 0.7 copy-done.1
  0.7 4.4 %sort.17 = (s32[1024]{0:T(1024)}, s32[1024]{0:T(1024)S(1)}) sort(s32[1024]{0:T(1024)S(1)} %copy-done.1, s32[1024]{0:T(1024)S(1)} %iota.35), dimensions={0}, to_apply=%region_0.0 | sort | flops 10240 | bytes 16384 | tf_op jit(solution)/shard_map/jit(argsort)/sort | solution.py:22
  5.1 4.5 %gather_fusion = s32[1024]{0:T(1024)S(1)} fusion(s32[1024]{0:T(1024)S(1)} %copy-done.1, s32[1024]{0:T(1024)S(1)} %fusion.25), kind=kCustom, calls=%fused_computation | custom fusion | bytes 12288 | tf_op jit(solution)/shard_map/gather | solution.py:23
  10.2 8.6 %gather_fusion.1 = s32[2048]{0:T(1024)S(1)} fusion(s32[1024]{0:T(1024)S(1)} %gather_fusion, s32[2048]{0:T(1024)S(1)} %broadcast_clamp_fusion.1), kind=kCustom, calls=%fused_computation.1 | custom fusion | bytes 24576 | tf_op jit(solution)/shard_map/gather | solution.py:34
  18.9 0.7 subtract_select_fusion
  19.6 7.1 %all-to-all-start = ((s32[32,64,1]{1,2,0:T(1,128)}), s32[32,64,1]{1,2,0:T(1,128)S(1)}, u32[]{:S(2)}, u32[]{:S(2)}) async-start(s32[32,64,1]{1,2,0:T(1,128)} %bitcast.4), calls=%async_computation | async-start | bytes 32768 | tf_op jit(solution)/shard_map/all_to_all | solution.py:38
  26.6 8.6 %gather_fusion.2 = s32[2048]{0:T(1024)S(1)} fusion(s32[1024]{0:T(1024)S(1)} %get-tuple-element.53, s32[2048]{0:T(1024)S(1)} %broadcast_clamp_fusion.1), kind=kCustom, calls=%fused_computation.2 | custom fusion | bytes 24576 | tf_op jit(solution)/shard_map/gather | solution.py:33
  35.3 8.0 %gather_fusion.3 = bf16[2048,128]{1,0:T(8,128)(2,1)} fusion(bf16[1024,128]{1,0:T(8,128)(2,1)S(1)} %copy-done, s32[2048]{0:T(1024)S(1)} %broadcast_clamp_fusion), kind=kCustom, calls=%fused_computation.3 | custom fusion | bytes 1056768 | tf_op jit(solution)/shard_map/gather | solution.py:35
  43.3 5.8 %all-to-all-start.1 = ((bf16[32,64,128]{2,1,0:T(8,128)(2,1)}), bf16[32,64,128]{2,1,0:T(8,128)(2,1)S(1)}, u32[]{:S(2)}, u32[]{:S(2)}) async-start(bf16[32,64,128]{2,1,0:T(8,128)(2,1)} %bitcast.8), calls=%async_computation.1 | async-start | bytes 1048576 | tf_op jit(solution)/shard_map/all_to_all | solution.py:37
  49.7 0.7 reduce.4
  50.5 13.9 %all-to-all-done.1 = bf16[32,64,128]{2,1,0:T(8,128)(2,1)S(1)} async-done(((bf16[32,64,128]{2,1,0:T(8,128)(2,1)}), bf16[32,64,128]{2,1,0:T(8,128)(2,1)S(1)}, u32[]{:S(2)}, u32[]{:S(2)}) %all-to-all-start.1) | async-done | bytes 524320 | tf_op jit(solution)/shard_map/all_to_all | solution.py:37
  64.3 5.7 %scatter_custom_fusion = bf16[1055,128]{1,0:T(8,128)(2,1)S(1)} fusion(s32[2048]{0:T(1024)S(1)} %bitcast.32, bf16[2048,128]{1,0:T(8,128)(2,1)S(1)} %bitcast.29, bf16[]{:T(256)} %constant.27.clone.1), kind=kCustom, calls=%fused_computation.25 | custom fusion | bytes 270082 | tf_op jit(solution)/shard_map/scatter | solution.py:41
  70.1 2.6 %collective-permute-start = (bf16[31,128]{1,0:T(8,128)(2,1)S(1)}, bf16[31,128]{1,0:T(8,128)(2,1)S(1)}, u32[]{:S(2)}, u32[]{:S(2)}) collective-permute-start(bf16[31,128]{1,0:T(8,128)(2,1)S(1)} %slice.26), channel_id=1, source_target_pairs={{1,0},{2,1},{3,2},{4,3},{5,4},{6,5},{7,6},{8,7},{9,8},{10,9},{11,1... | collective-permute-start | bytes 23816 | tf_op jit(solution)/shard_map/ppermute | solution.py:12
  72.7 2.3 %collective-permute-done = bf16[31,128]{1,0:T(8,128)(2,1)S(1)} collective-permute-done((bf16[31,128]{1,0:T(8,128)(2,1)S(1)}, bf16[31,128]{1,0:T(8,128)(2,1)S(1)}, u32[]{:S(2)}, u32[]{:S(2)}) %collective-permute-start) | collective-permute-done | bytes 7968 | tf_op jit(solution)/shard_map/ppermute | solution.py:12
  75.1 0.6 copy-done.3
  75.8 101.2 %while.11 = (s32[]{:T(128)}, f32[31,1024]{1,0:T(8,128)S(1)}, s32[31]{0:T(128)S(1)}, bf16[1055,128]{1,0:T(8,128)(2,1)S(1)}, f32[1024,128]{1,0:T(8,128)S(1)}, /*in...) while((s32[]{:T(128)}, f32[31,1024]{1,0:T(8,128)S(1)}, ...), condition=%wide.region_5.6_spmd.clone, body=%wide.region_4.5_spmd.sunk.clone | while | flops 68812800 | bytes 2700439 | solution.py:64
  82.3 0.6 dynamic_slice.24
  85.5 0.6 dynamic_slice.24
  88.8 0.6 dynamic_slice.24
  92.0 0.6 dynamic_slice.24
  95.3 0.6 dynamic_slice.24
  101.8 0.6 dynamic_slice.24
  105.1 0.6 dynamic_slice.24
  111.6 0.6 dynamic_slice.24
  114.9 0.6 dynamic_slice.24
  118.2 0.6 dynamic_slice.24
  121.4 0.6 dynamic_slice.24
  124.7 0.6 dynamic_slice.24
  128.0 0.6 dynamic_slice.24
  137.8 0.6 dynamic_slice.24
  141.0 0.6 dynamic_slice.24
  177.0 0.7 fusion.23
  (143 shorter events, 32.8 us)
Async XLA Ops:
  0.0 35.3 %copy-start = (bf16[1024,128]{1,0:T(8,128)(2,1)S(1)}, bf16[1024,128]{1,0:T(8,128)(2,1)}, u32[]{:S(2)}) copy-start(bf16[1024,128]{1,0:T(8,128)(2,1)} %param.7) | copy-start | bytes 786436
  0.0 0.7 copy-start.1
  19.6 23.7 %all-to-all-start = ((s32[32,64,1]{1,2,0:T(1,128)}), s32[32,64,1]{1,2,0:T(1,128)S(1)}, u32[]{:S(2)}, u32[]{:S(2)}) async-start(s32[32,64,1]{1,2,0:T(1,128)} %bitcast.4), calls=%async_computation | async-start | bytes 32768 | tf_op jit(solution)/shard_map/all_to_all | solution.py:38
  43.3 5.9 %copy-start.2 = (bf16[256,128]{1,0:T(8,128)(2,1)S(1)}, bf16[256,128]{1,0:T(8,128)(2,1)}, u32[]{:S(2)}) copy-start(bf16[256,128]{1,0:T(8,128)(2,1)} %param.9) | copy-start | bytes 196612
  43.3 21.1 %all-to-all-start.1 = ((bf16[32,64,128]{2,1,0:T(8,128)(2,1)}), bf16[32,64,128]{2,1,0:T(8,128)(2,1)S(1)}, u32[]{:S(2)}, u32[]{:S(2)}) async-start(bf16[32,64,128]{2,1,0:T(8,128)(2,1)} %bitcast.8), calls=%async_computation.1 | async-start | bytes 1048576 | tf_op jit(solution)/shard_map/all_to_all | solution.py:37
  70.1 5.0 %collective-permute-start = (bf16[31,128]{1,0:T(8,128)(2,1)S(1)}, bf16[31,128]{1,0:T(8,128)(2,1)S(1)}, u32[]{:S(2)}, u32[]{:S(2)}) collective-permute-start(bf16[31,128]{1,0:T(8,128)(2,1)S(1)} %slice.26), channel_id=1, source_target_pairs={{1,0},{2,1},{3,2},{4,3},{5,4},{6,5},{7,6},{8,7},{9,8},{10,9},{11,1... | collective-permute-start | bytes 23816 | tf_op jit(solution)/shard_map/ppermute | solution.py:12
  75.1 0.7 copy-start.3
  75.1 0.7 copy-start.4
where the time goes:
time: 179 us; the launch traced here: 178 us
  loops' own time  61.1 us (34%)
  local copies, waits for them, and re-layouts  58.5 us (33%)
  matrix products  19.3 us (11%)
  waiting for transfers between devices  16.2 us (9%)
  starting transfers between devices  15.5 us (9%)
  other arithmetic  6.99 us (4%)
    another operation x1, loops' own time, body(): scores = lax.map(score_offset, offsets)  61.1 us
    dynamic_slice x31, local copies, waits for them, and re-layouts, body(): scores = lax.map(score_offset, offsets)  18.2 us
    all_to_all x1, waiting for transfers between devices, body(): lax.all_to_all(outgoing, 'dev', split_axis=0, concat_axis=0, tiled=True)  13.9 us
    dot_general x31, matrix products, score_offset(): return jnp.dot(hidden, score_weight, preferred_element_type=jnp.float32)  12.1 us
    gather x2, local copies, waits for them, and re-layouts, body(): ranked[slot_index] - owner_ids[:, None] * rows_dev  8.66 us
    gather x1, local copies, waits for them, and re-layouts, body(): source_rows = by_rank[slot_index]  8.58 us
    gather x1, local copies, waits for them, and re-layouts, body(): outgoing = embeddings[source_rows.reshape(-1)]  7.97 us
    dot_general x31, matrix products, score_offset(): jnp.dot(product, weight_product, preferred_element_type=jnp.float32)  7.16 us
  transfers between devices with their start and end apart: 3, of which 2 were waited for; matrix products, arithmetic and copies ran while one was open for 10% of the time, Pallas kernels for 0%

commit v1 on v0

v1 whole, which is shorter than its diff:
```python
import functools

import jax
import jax.numpy as jnp
from jax import lax
from jax.experimental import pallas as pl
from jax.experimental.pallas import tpu as pltpu
from jax.sharding import PartitionSpec as P

WIN = 32
LANES = 128
CHUNK = 256
VMEM = pl.BlockSpec(memory_space=pltpu.VMEM)
SMEM = pl.BlockSpec(memory_space=pltpu.SMEM)


def one_hot(values, count):
    index = lax.broadcasted_iota(jnp.int32, (count, 1), 0).astype(jnp.float32)
    hit = values.astype(jnp.bfloat16) == index.astype(jnp.bfloat16)
    return jnp.where(hit, jnp.bfloat16(1), jnp.bfloat16(0))


def in_chunk(values, chunk):
    local = values - chunk * CHUNK
    return jnp.where((local >= 0) & (local < CHUNK), local, -1)


def pack_kernel(ranks_ref, rows_ref, out_ref, *, devices, capacity):
    count = rows_ref.shape[0]
    ranks = ranks_ref[...]
    owner = ranks // count
    position = ranks - owner * count
    high = (position // CHUNK + 1).astype(jnp.float32)
    low = (position % CHUNK).astype(jnp.float32)

    device_ids = lax.broadcasted_iota(jnp.int32, (devices, 1), 0)
    before = (
        lax.broadcasted_iota(jnp.int32, (CHUNK, CHUNK), 0)
        < lax.broadcasted_iota(jnp.int32, (CHUNK, CHUNK), 1)
    )
    before = jnp.where(before, 1.0, 0.0).astype(jnp.bfloat16)
    offset = jnp.zeros((devices, 1), jnp.float32)
    slots = []
    for start in range(0, count, CHUNK):
        member = jnp.where(device_ids == owner[:, start : start + CHUNK], 1.0, 0.0)
        earlier = jnp.dot(
            member.astype(jnp.bfloat16), before, preferred_element_type=jnp.float32
        )
        slots.append(jnp.sum(member * (earlier + offset), axis=0, keepdims=True))
        offset = offset + jnp.sum(member, axis=1, keepdims=True)
    slot = jnp.concatenate(slots, axis=1)
    target = owner * capacity + slot.astype(jnp.int32)

    rows = rows_ref[...]
    group = CHUNK // capacity
    for chunk in range(devices * capacity // CHUNK):
        pick = one_hot(in_chunk(target, chunk), CHUNK)
        packed = jnp.dot(pick, rows, preferred_element_type=jnp.float32)
        out_ref[chunk * group : (chunk + 1) * group, :capacity, :] = packed.reshape(
            group, capacity, LANES
        ).astype(jnp.bfloat16)

    lane = lax.broadcasted_iota(jnp.int32, (LANES, 1), 0) % capacity
    spot = jnp.where(slot.astype(jnp.int32) == lane, 1.0, 0.0).astype(jnp.bfloat16)
    line = lax.broadcasted_iota(jnp.int32, (devices * 8, 1), 0)
    kind = line % 8
    value = jnp.where(kind == 0, high, jnp.where(kind == 1, low, 0.0))
    value = jnp.where(line // 8 == owner, value, 0.0).astype(jnp.bfloat16)
    places = lax.dot_general(
        value, spot, (((1,), (1,)), ((), ())), preferred_element_type=jnp.float32
    )
    out_ref[:, capacity:, :] = places.reshape(devices, 8, LANES).astype(jnp.bfloat16)


def sort_kernel(arrived_ref, wide_ref, narrow_ref, head_ref, *, capacity):
    devices = arrived_ref.shape[0]
    share = LANES // capacity
    lane = lax.broadcasted_iota(jnp.int32, (8, LANES), 1)
    highs, lows = [], []
    for first in range(0, devices, share):
        places = arrived_ref[first, capacity:, :].astype(jnp.float32)
        for step in range(1, share):
            other = arrived_ref[first + step, capacity:, :].astype(jnp.float32)
            places = jnp.where(lane >= step * capacity, other, places)
        highs.append(places[0:1])
        lows.append(places[1:2])
    high = jnp.concatenate(highs, axis=1)
    low = jnp.concatenate(lows, axis=1)
    rows = arrived_ref[:, :capacity, :].reshape(devices * capacity, LANES)
    for chunk in range(wide_ref.shape[0] // CHUNK):
        pick = one_hot(jnp.where(high == chunk + 1, low, -1.0), CHUNK)
        ordered = jnp.dot(pick, rows, preferred_element_type=jnp.float32)
        wide_ref[chunk * CHUNK : (chunk + 1) * CHUNK, :] = ordered
        narrow_ref[chunk * CHUNK : (chunk + 1) * CHUNK, :] = ordered.astype(jnp.bfloat16)
        if chunk == 0:
            head_ref[...] = ordered[:WIN].astype(jnp.bfloat16)


def score_block(leading, wide_ref, start, offset, weight, bias_ref, score_ref):
    partner = wide_ref[pl.ds(start + offset, CHUNK), :].astype(jnp.bfloat16)
    features = jnp.concatenate([leading * partner, jnp.abs(leading - partner)], axis=1)
    hidden = lax.dot_general(
        weight, features, (((1,), (1,)), ((), ())), preferred_element_type=jnp.float32
    )
    hidden = jnp.maximum(hidden + bias_ref[...], 0.0) * score_ref[...]
    return jnp.sum(hidden, axis=0, keepdims=True)


def main_kernel(wide_ref, narrow_ref, weight_ref, bias_ref, score_ref, out_ref):
    weight = weight_ref[...]

    def step(offset, carry):
        for start in range(0, out_ref.shape[1], CHUNK):
            leading = narrow_ref[start : start + CHUNK, :]
            out_ref[pl.ds(offset - 1, 1), start : start + CHUNK] = score_block(
                leading, wide_ref, start, offset, weight, bias_ref, score_ref
            )
        return carry

    lax.fori_loop(1, WIN, step, 0)


def tail_kernel(
    limit_ref, wide_ref, narrow_ref, next_ref, weight_ref, bias_ref, score_ref, _, out_ref,
    joined_ref,
):
    weight = weight_ref[...]
    count = wide_ref.shape[0]
    base = count - CHUNK
    joined_ref[:CHUNK, :] = wide_ref[base:, :]
    joined_ref[CHUNK:, :] = next_ref[...].astype(jnp.float32)
    leading = narrow_ref[base:, :]
    place = base + lax.broadcasted_iota(jnp.int32, (1, CHUNK), 1)
    limit = limit_ref[0]

    def step(offset, carry):
        line = score_block(leading, joined_ref, 0, offset, weight, bias_ref, score_ref)
        out_ref[pl.ds(offset - 1, 1), :] = jnp.where(place + offset < limit, line, 0.0)
        return carry

    lax.fori_loop(1, WIN, step, 0)


def body(embeddings, ranks, pair_weight, pair_bias, score_weight):
    rows_dev, width = embeddings.shape
    devices = lax.axis_size("dev")
    capacity = 2 * rows_dev // devices
    hidden = pair_weight.shape[1]

    outgoing = pl.pallas_call(
        functools.partial(pack_kernel, devices=devices, capacity=capacity),
        out_shape=jax.ShapeDtypeStruct((devices, capacity + 8, width), jnp.bfloat16),
        in_specs=[VMEM] * 2,
        out_specs=VMEM,
        name="pack",
    )(ranks.reshape(1, rows_dev), embeddings)
    arrived = lax.all_to_all(outgoing, "dev", split_axis=0, concat_axis=0, tiled=True)
    weight = pair_weight.T
    bias = jnp.broadcast_to(pair_bias[:, None], (hidden, CHUNK))
    score = jnp.broadcast_to(score_weight.astype(jnp.float32)[:, None], (hidden, CHUNK))

    wide, narrow, head = pl.pallas_call(
        functools.partial(sort_kernel, capacity=capacity),
        out_shape=(
            jax.ShapeDtypeStruct((rows_dev, width), jnp.float32),
            jax.ShapeDtypeStruct((rows_dev, width), jnp.bfloat16),
            jax.ShapeDtypeStruct((WIN, width), jnp.bfloat16),
        ),
        in_specs=[VMEM],
        out_specs=(VMEM, VMEM, VMEM),
        name="sort",
    )(arrived)
    following = lax.ppermute(head, "dev", [(i, i - 1) for i in range(1, devices)])

    pairs = (WIN - 1) * rows_dev
    scores = pl.pallas_call(
        main_kernel,
        grid=(1,),
        out_shape=jax.ShapeDtypeStruct((WIN - 1, rows_dev), jnp.float32),
        in_specs=[VMEM] * 5,
        out_specs=pl.BlockSpec((WIN - 1, rows_dev - CHUNK), lambda i: (0, 0)),
        cost_estimate=pl.CostEstimate(
            flops=4 * pairs * width * hidden, bytes_accessed=4 * pairs, transcendentals=0
        ),
        name="main",
    )(wide, narrow, weight, bias, score)
    last = lax.axis_index("dev") == devices - 1
    limit = jnp.where(last, rows_dev, 2 * rows_dev).astype(jnp.int32).reshape(1)
    return pl.pallas_call(
        tail_kernel,
        grid=(1,),
        out_shape=jax.ShapeDtypeStruct((WIN - 1, rows_dev), jnp.float32),
        in_specs=[SMEM] + [VMEM] * 6 + [pl.BlockSpec(memory_space=pl.ANY)],
        out_specs=pl.BlockSpec((WIN - 1, CHUNK), lambda i: (0, rows_dev // CHUNK - 1)),
        scratch_shapes=[pltpu.VMEM((CHUNK + WIN, width), jnp.float32)],
        input_output_aliases={7: 0},
        name="tail",
    )(limit, wide, narrow, following, weight, bias, score, scores)


def solution(mesh):
    placed = (P("dev", None), P("dev"), P(), P(), P())
    return jax.shard_map(
        body, mesh=mesh, in_specs=placed, out_specs=P(None, "dev"), check_vma=False
    )
```

time: 179 us -> 57.8 us (0.32)
  loops' own time: 61.1 us -> 0 us
  local copies, waits for them, and re-layouts: 58.5 us -> 4.28 us
  Pallas kernels: 0 us -> 27.8 us
  matrix products: 19.3 us -> 0 us
  other arithmetic: 6.99 us -> 0 us
  starting transfers between devices: 15.5 us -> 9.5 us
    another operation x1 -> x0, loops' own time: 61.1 us -> none  [body(): scores = lax.map(score_offset, offsets)]
    gather x5 -> x0, local copies, waits for them, and re-layouts: 29.7 us -> none  [the longest x2 8.66 us: body(): ranked[slot_index] - owner_ids[:, None] * rows_dev]
    pallas_call x0 -> x4, Pallas kernels: none -> 27.8 us  [the longest x1 12 us: body(): pl.pallas_call(main_kernel, grid=(1,), out_shape=jax.ShapeDtypeStruct((WI...]
    dot_general x62 -> x0, matrix products: 19.3 us -> none  [the longest x31 12.1 us: score_offset(): return jnp.dot(hidden, score_weight, preferred_element_type=jnp.float32)]
    dynamic_slice x31 -> x0, local copies, waits for them, and re-layouts: 18.2 us -> none  [body(): scores = lax.map(score_offset, offsets)]
    all_to_all x1 -> x0, starting transfers between devices: 7.08 us -> none  [body(): lax.all_to_all(target.reshape(-1), 'dev', split_axis=0, concat_axis=0, ti...]
    scatter x1 -> x0, local copies, waits for them, and re-layouts: 5.74 us -> none  [body(): jnp.zeros((rows_dev + margin, width), jnp.bfloat16).at[positions]]
    sort x1 -> x0, other arithmetic: 4.36 us -> none  [body(): by_rank = jnp.argsort(ranks)]
  transfers between devices with their start and end apart: 3 -> 2, of which waited for: 2 -> 1; matrix products, arithmetic and copies ran while one was open for 10% -> 4% of each run, Pallas kernels for 0% -> 21%
where the time goes in v1:
time: 57.8 us; the launch traced here: 57.4 us
  Pallas kernels  27.8 us (48%)
  waiting for transfers between devices  15.8 us (27%)
  starting transfers between devices  9.5 us (16%)
  local copies, waits for them, and re-layouts  4.28 us (7%)
    all_to_all x1, waiting for transfers between devices, body(): lax.all_to_all(outgoing, 'dev', split_axis=0, concat_axis=0, tiled=True)  15.8 us
    pallas_call x1, Pallas kernels, body(): pl.pallas_call(main_kernel, grid=(1,), out_shape=jax.ShapeDtypeStruct((WI...  12 us
    pallas_call x1, Pallas kernels, body(): pl.pallas_call(tail_kernel, grid=(1,), out_shape=jax.ShapeDtypeStruct((WI...  9.17 us
    all_to_all x1, starting transfers between devices, body(): lax.all_to_all(outgoing, 'dev', split_axis=0, concat_axis=0, tiled=True)  7.08 us
    pallas_call x1, Pallas kernels, body(): pl.pallas_call(functools.partial(pack_kernel, devices=devices, capacity=c...  3.4 us
    pallas_call x1, Pallas kernels, body(): pl.pallas_call(functools.partial(sort_kernel, capacity=capacity), out_sha...  3.22 us
    unnamed x11, local copies, waits for them, and re-layouts  2.81 us
    ppermute x1, starting transfers between devices, body(): lax.ppermute(head, 'dev', [(i, i - 1) for i in range(1, devices)])  2.41 us
  transfers between devices with their start and end apart: 2, of which 1 were waited for; matrix products, arithmetic and copies ran while one was open for 4% of the time, Pallas kernels for 21%

profile of v1, /device:TPU:1, one launch (start us, length us, event | category | flops | bytes accessed | tf_op | source)
XLA Modules:
  0.0 57.4 jit_solution(2057056486109413917)
XLA Ops:
  0.0 3.4 %pack.1 = bf16[32,72,128]{2,1,0:T(8,128)(2,1)} custom-call(s32[1,1024]{1,0:T(1,128)} %bitcast.5, bf16[1024,128]{1,0:T(8,128)(2,1)} %rows_ref.1), custom_call_target="tpu_custom_call" | custom-call | tf_op jit(solution)/shard_map/pack/pallas_call | solution.py:150
  3.4 0.0 copy-start.1
  3.4 7.1 %all-to-all-start = ((bf16[32,72,128]{2,1,0:T(8,128)(2,1)}), bf16[32,72,128]{2,1,0:T(8,128)(2,1)S(1)}, u32[]{:S(2)}, u32[]{:S(2)}) async-start(bf16[32,72,128]{2,1,0:T(8,128)(2,1)} %pack.1), calls=%async_computation | async-start | bytes 1179648 | tf_op jit(solution)/shard_map/all_to_all | solution.py:157
  10.5 0.0 copy-done.1
  10.5 0.7 %copy.7 = bf16[256,128]{0,1:T(8,128)(2,1)} copy(bf16[256,128]{1,0:T(8,128)(2,1)S(1)} %copy-done.1) | data formatting | bytes 131072 | tf_op args[2]
  11.2 15.8 %all-to-all-done.arrived_ref = bf16[32,72,128]{2,1,0:T(8,128)(2,1)S(1)} async-done(((bf16[32,72,128]{2,1,0:T(8,128)(2,1)}), bf16[32,72,128]{2,1,0:T(8,128)(2,1)S(1)}, u32[]{:S(2)}, u32[]{:S(2)}) %all-to-all-start) | async-done | bytes 589856 | tf_op jit(solution)/shard_map/all_to_all | solution.py:157
  27.0 0.0 copy-start
  27.0 0.8 %copy-done = bf16[32,72,128]{2,1,0:T(8,128)(2,1)} copy-done((bf16[32,72,128]{2,1,0:T(8,128)(2,1)}, bf16[32,72,128]{2,1,0:T(8,128)(2,1)S(1)}, u32[]{:S(2)}) %copy-start) | copy-done | bytes 589848
  27.9 3.2 %sort.1 = (f32[1024,128]{1,0:T(8,128)}, bf16[1024,128]{1,0:T(8,128)(2,1)}, bf16[32,128]{1,0:T(8,128)(2,1)}) custom-call(bf16[32,72,128]{2,1,0:T(8,128)(2,1)} %copy-done), custom_call_target="tpu_custom_call" | custom-call | tf_op jit(solution)/shard_map/sort/pallas_call | solution.py:162
  31.1 2.4 %collective-permute-start = (bf16[32,128]{1,0:T(8,128)(2,1)}, bf16[32,128]{1,0:T(8,128)(2,1)S(1)}, u32[]{:S(2)}, u32[]{:S(2)}) collective-permute-start(bf16[32,128]{1,0:T(8,128)(2,1)} %get-tuple-element.10), channel_id=1, source_target_pairs={{1,0},{2,1},{3,2},{4,3},{5,4},{6,5},{7,6},{8,7},{9,8},{10,9},{11,1... | collective-permute-start | bytes 24584 | tf_op jit(solution)/shard_map/ppermute | solution.py:173
  33.5 0.0 copy-start.3
  33.5 0.6 %copy-done.3 = f32[128]{0:T(128)S(1)} copy-done((f32[128]{0:T(128)S(1)}, f32[128]{0:T(128)}, u32[]{:S(2)}) %copy-start.3) | copy-done | bytes 536
  34.1 0.0 copy-start.4
  34.2 0.7 %broadcast_in_dim.4.bias_ref = f32[128,256]{1,0:T(8,128)} broadcast(f32[128]{0:T(128)S(1)} %copy-done.3), dimensions={0} | broadcast | bytes 131584 | tf_op jit(solution)/shard_map/broadcast_in_dim | solution.py:159
  34.9 0.0 copy-done.4
  34.9 0.7 %broadcast_in_dim.5.score_ref = f32[128,256]{1,0:T(8,128)} broadcast(bf16[128]{0:T(256)(128)(2,1)S(1)} %copy-done.4), dimensions={0} | broadcast | bytes 131328 | tf_op jit(solution)/shard_map/broadcast_in_dim | solution.py:160
  35.6 12.0 %main.1._ = f32[31,1024]{1,0:T(8,128)} custom-call(f32[1024,128]{1,0:T(8,128)} %get-tuple-element.8.wide_ref, bf16[1024,128]{1,0:T(8,128)(2,1)} %get-tuple-element.9.narrow_ref, bf16[128,256]{1,0:T(8,128)(2,1)} %bitcast.3, f32[128,256]{1,0:T(8,128)} %broadcast_in_dim.4.bias_ref, f32[128,256]{1,0:T(8,128)} %broadcast_in_dim.5.score_ref), custom_call_target="tpu_custom_call" | custom-call | flops 2080374784 | bytes 126976 | tf_op jit(solution)/shard_map/main/pallas_call | solution.py:176
  47.6 0.0 collective-permute-done.next_ref
  47.6 0.0 copy-start.2
  47.7 0.6 %copy-done.2 = bf16[32,128]{1,0:T(8,128)(2,1)} copy-done((bf16[32,128]{1,0:T(8,128)(2,1)}, bf16[32,128]{1,0:T(8,128)(2,1)S(1)}, u32[]{:S(2)}) %copy-start.2) | copy-done | bytes 8216
  48.2 9.2 %tail.1 = f32[31,1024]{1,0:T(8,128)} custom-call(s32[1]{0:T(128)} %bitcast.limit_ref, f32[1024,128]{1,0:T(8,128)} %get-tuple-element.8.wide_ref, bf16[1024,128]{1,0:T(8,128)(2,1)} %get-tuple-element.9.narrow_ref, bf16[32,128]{1,0:T(8,128)(2,1)} %copy-done.2, bf16[128,256]{1,0:T(8,128)(2,1)} %bitcast.4, ...), custom_call_target="tpu_custom_call", output_to_operand_aliasing={{}: (7, {})} | custom-call | tf_op jit(solution)/shard_map/tail/pallas_call | solution.py:189
Async XLA Ops:
  3.4 7.1 %copy-start.1 = (bf16[256,128]{1,0:T(8,128)(2,1)S(1)}, bf16[256,128]{1,0:T(8,128)(2,1)}, u32[]{:S(2)}) copy-start(bf16[256,128]{1,0:T(8,128)(2,1)} %param.7) | copy-start | bytes 196612
  3.4 23.6 %all-to-all-start = ((bf16[32,72,128]{2,1,0:T(8,128)(2,1)}), bf16[32,72,128]{2,1,0:T(8,128)(2,1)S(1)}, u32[]{:S(2)}, u32[]{:S(2)}) async-start(bf16[32,72,128]{2,1,0:T(8,128)(2,1)} %pack.1), calls=%async_computation | async-start | bytes 1179648 | tf_op jit(solution)/shard_map/all_to_all | solution.py:157
  27.0 0.8 %copy-start = (bf16[32,72,128]{2,1,0:T(8,128)(2,1)}, bf16[32,72,128]{2,1,0:T(8,128)(2,1)S(1)}, u32[]{:S(2)}) copy-start(bf16[32,72,128]{2,1,0:T(8,128)(2,1)S(1)} %all-to-all-done.arrived_ref) | copy-start | bytes 1769476
  31.1 16.6 %collective-permute-start = (bf16[32,128]{1,0:T(8,128)(2,1)}, bf16[32,128]{1,0:T(8,128)(2,1)S(1)}, u32[]{:S(2)}, u32[]{:S(2)}) collective-permute-start(bf16[32,128]{1,0:T(8,128)(2,1)} %get-tuple-element.10), channel_id=1, source_target_pairs={{1,0},{2,1},{3,2},{4,3},{5,4},{6,5},{7,6},{8,7},{9,8},{10,9},{11,1... | collective-permute-start | bytes 24584 | tf_op jit(solution)/shard_map/ppermute | solution.py:173
  33.5 0.7 %copy-start.3 = (f32[128]{0:T(128)S(1)}, f32[128]{0:T(128)}, u32[]{:S(2)}) copy-start(f32[128]{0:T(128)} %param.8) | copy-start | bytes 1540
  34.1 0.7 %copy-start.4 = (bf16[128]{0:T(256)(128)(2,1)S(1)}, bf16[128]{0:T(256)(128)(2,1)}, u32[]{:S(2)}) copy-start(bf16[128]{0:T(256)(128)(2,1)} %param.9) | copy-start | bytes 772
  47.6 0.6 %copy-start.2 = (bf16[32,128]{1,0:T(8,128)(2,1)}, bf16[32,128]{1,0:T(8,128)(2,1)S(1)}, u32[]{:S(2)}) copy-start(bf16[32,128]{1,0:T(8,128)(2,1)S(1)} %collective-permute-done.next_ref) | copy-start | bytes 24580

commit v2 on v1

--- a/solution.py
+++ b/solution.py
@@ -12,6 +12,8 @@
 CHUNK = 256
 VMEM = pl.BlockSpec(memory_space=pltpu.VMEM)
 SMEM = pl.BlockSpec(memory_space=pltpu.SMEM)
+ANY = pl.BlockSpec(memory_space=pl.ANY)
+SMALL = pltpu.CompilerParams(vmem_limit_bytes=16 * 2**20)
 
 
 def one_hot(values, count):
@@ -72,7 +74,8 @@
     out_ref[:, capacity:, :] = places.reshape(devices, 8, LANES).astype(jnp.bfloat16)
 
 
-def sort_kernel(arrived_ref, wide_ref, narrow_ref, head_ref, *, capacity):
+def sort_kernel(arrived_ref, *refs, capacity):
+    wide_ref, head_ref = refs[-2:]
     devices = arrived_ref.shape[0]
     share = LANES // capacity
     lane = lax.broadcasted_iota(jnp.int32, (8, LANES), 1)
@@ -91,54 +94,71 @@
         pick = one_hot(jnp.where(high == chunk + 1, low, -1.0), CHUNK)
         ordered = jnp.dot(pick, rows, preferred_element_type=jnp.float32)
         wide_ref[chunk * CHUNK : (chunk + 1) * CHUNK, :] = ordered
-        narrow_ref[chunk * CHUNK : (chunk + 1) * CHUNK, :] = ordered.astype(jnp.bfloat16)
         if chunk == 0:
             head_ref[...] = ordered[:WIN].astype(jnp.bfloat16)
 
 
-def score_block(leading, wide_ref, start, offset, weight, bias_ref, score_ref):
-    partner = wide_ref[pl.ds(start + offset, CHUNK), :].astype(jnp.bfloat16)
+def prepare_kernel(weight_ref, bias_ref, score_ref, turned_ref, floor_ref, scale_ref, base_ref):
+    turned_ref[...] = weight_ref[...].astype(jnp.float32).T.astype(jnp.bfloat16)
+    bias = bias_ref[...]
+    score = score_ref[...].astype(jnp.float32)
+    hidden = bias.shape[1]
+    floor = jnp.broadcast_to(-bias, (CHUNK, hidden)).T
+    floor_ref[...] = floor
+    scale_ref[...] = jnp.broadcast_to(score, (CHUNK, hidden)).T
+    base_ref[...] = jnp.broadcast_to(
+        jnp.sum(bias * score, axis=1, keepdims=True), base_ref.shape
+    )
+
+
+def score_tile(leading, partner, weight, floor_ref, scale_ref, base_ref):
     features = jnp.concatenate([leading * partner, jnp.abs(leading - partner)], axis=1)
     hidden = lax.dot_general(
         weight, features, (((1,), (1,)), ((), ())), preferred_element_type=jnp.float32
     )
-    hidden = jnp.maximum(hidden + bias_ref[...], 0.0) * score_ref[...]
-    return jnp.sum(hidden, axis=0, keepdims=True)
-
-
-def main_kernel(wide_ref, narrow_ref, weight_ref, bias_ref, score_ref, out_ref):
-    weight = weight_ref[...]
-
-    def step(offset, carry):
-        for start in range(0, out_ref.shape[1], CHUNK):
-            leading = narrow_ref[start : start + CHUNK, :]
-            out_ref[pl.ds(offset - 1, 1), start : start + CHUNK] = score_block(
-                leading, wide_ref, start, offset, weight, bias_ref, score_ref
-            )
-        return carry
-
-    lax.fori_loop(1, WIN, step, 0)
+    hidden = jnp.maximum(hidden, floor_ref[...]) * scale_ref[...]
+    return jnp.sum(hidden, axis=0, keepdims=True) + base_ref[...]
+
+
+def score_blocks(blocks, wide_ref, write, parameters):
+    weight = parameters[0][...]
+    half = WIN // 2
+    leadings = [wide_ref[b * CHUNK : (b + 1) * CHUNK, :].astype(jnp.bfloat16) for b in range(blocks)]
+    for offset in range(1, half + 1):
+        for b in range(blocks):
+            first = b * CHUNK + offset
+            extra = half if offset < half else 0
+            partner = wide_ref[first : first + CHUNK + extra, :].astype(jnp.bfloat16)
+            for add in (0, half)[: 2 if extra else 1]:
+                line = score_tile(
+                    leadings[b], partner[add : add + CHUNK], weight, *parameters[1:]
+                )
+                write(offset + add, b, line)
+
+
+def main_kernel(wide_ref, turned_ref, floor_ref, scale_ref, base_ref, out_ref):
+    def write(offset, block, line):
+        out_ref[offset - 1 : offset, block * CHUNK : (block + 1) * CHUNK] = line
+
+    score_blocks(
+        out_ref.shape[1] // CHUNK, wide_ref, write, (turned_ref, floor_ref, scale_ref, base_ref)
+    )
 
 
 def tail_kernel(
-    limit_ref, wide_ref, narrow_ref, next_ref, weight_ref, bias_ref, score_ref, _, out_ref,
+    limit_ref, wide_ref, next_ref, turned_ref, floor_ref, scale_ref, base_ref, _, out_ref,
     joined_ref,
 ):
-    weight = weight_ref[...]
     count = wide_ref.shape[0]
-    base = count - CHUNK
-    joined_ref[:CHUNK, :] = wide_ref[base:, :]
+    joined_ref[:CHUNK, :] = wide_ref[count - CHUNK :, :]
     joined_ref[CHUNK:, :] = next_ref[...].astype(jnp.float32)
-    leading = narrow_ref[base:, :]
-    place = base + lax.broadcasted_iota(jnp.int32, (1, CHUNK), 1)
+    place = count - CHUNK + lax.broadcasted_iota(jnp.int32, (1, CHUNK), 1)
     limit = limit_ref[0]
 
-    def step(offset, carry):
-        line = score_block(leading, joined_ref, 0, offset, weight, bias_ref, score_ref)
-        out_ref[pl.ds(offset - 1, 1), :] = jnp.where(place + offset < limit, line, 0.0)
-        return carry
-
-    lax.fori_loop(1, WIN, step, 0)
+    def write(offset, block, line):
+        out_ref[offset - 1 : offset, :] = jnp.where(place + offset < limit, line, 0.0)
+
+    score_blocks(1, joined_ref, write, (turned_ref, floor_ref, scale_ref, base_ref))
 
 
 def body(embeddings, ranks, pair_weight, pair_bias, score_weight):
@@ -152,27 +172,38 @@
         out_shape=jax.ShapeDtypeStruct((devices, capacity + 8, width), jnp.bfloat16),
         in_specs=[VMEM] * 2,
         out_specs=VMEM,
+        compiler_params=SMALL,
         name="pack",
     )(ranks.reshape(1, rows_dev), embeddings)
     arrived = lax.all_to_all(outgoing, "dev", split_axis=0, concat_axis=0, tiled=True)
-    weight = pair_weight.T
-    bias = jnp.broadcast_to(pair_bias[:, None], (hidden, CHUNK))
-    score = jnp.broadcast_to(score_weight.astype(jnp.float32)[:, None], (hidden, CHUNK))
-
-    wide, narrow, head = pl.pallas_call(
+    parameters = pl.pallas_call(
+        prepare_kernel,
+        out_shape=(
+            jax.ShapeDtypeStruct((hidden, 2 * width), jnp.bfloat16),
+            jax.ShapeDtypeStruct((hidden, CHUNK), jnp.float32),
+            jax.ShapeDtypeStruct((hidden, CHUNK), jnp.float32),
+            jax.ShapeDtypeStruct((1, CHUNK), jnp.float32),
+        ),
+        in_specs=[VMEM] * 3,
+        out_specs=(VMEM,) * 4,
+        compiler_params=SMALL,
+        name="prepare",
+    )(pair_weight, pair_bias.reshape(1, hidden), score_weight.reshape(1, hidden))
+
+    wide, head = pl.pallas_call(
         functools.partial(sort_kernel, capacity=capacity),
         out_shape=(
             jax.ShapeDtypeStruct((rows_dev, width), jnp.float32),
-            jax.ShapeDtypeStruct((rows_dev, width), jnp.bfloat16),
             jax.ShapeDtypeStruct((WIN, width), jnp.bfloat16),
         ),
-        in_specs=[VMEM],
-        out_specs=(VMEM, VMEM, VMEM),
+        in_specs=[VMEM] + [ANY] * 4,
+        out_specs=(VMEM, VMEM),
+        compiler_params=SMALL,
         name="sort",
-    )(arrived)
+    )(arrived, *parameters)
     following = lax.ppermute(head, "dev", [(i, i - 1) for i in range(1, devices)])
 
-    pairs = (WIN - 1) * rows_dev
+    pairs = (WIN - 1) * (rows_dev - CHUNK)
     scores = pl.pallas_call(
         main_kernel,
         grid=(1,),
@@ -182,20 +213,22 @@
         cost_estimate=pl.CostEstimate(
             flops=4 * pairs * width * hidden, bytes_accessed=4 * pairs, transcendentals=0
         ),
+        compiler_params=SMALL,
         name="main",
-    )(wide, narrow, weight, bias, score)
+    )(wide, *parameters)
     last = lax.axis_index("dev") == devices - 1
     limit = jnp.where(last, rows_dev, 2 * rows_dev).astype(jnp.int32).reshape(1)
     return pl.pallas_call(
         tail_kernel,
         grid=(1,),
         out_shape=jax.ShapeDtypeStruct((WIN - 1, rows_dev), jnp.float32),
-        in_specs=[SMEM] + [VMEM] * 6 + [pl.BlockSpec(memory_space=pl.ANY)],
+        in_specs=[SMEM] + [VMEM] * 6 + [ANY],
         out_specs=pl.BlockSpec((WIN - 1, CHUNK), lambda i: (0, rows_dev // CHUNK - 1)),
         scratch_shapes=[pltpu.VMEM((CHUNK + WIN, width), jnp.float32)],
         input_output_aliases={7: 0},
+        compiler_params=SMALL,
         name="tail",
-    )(limit, wide, narrow, following, weight, bias, score, scores)
+    )(limit, wide, following, *parameters, scores)
 
 
 def solution(mesh):

time: 57.8 us -> 38.7 us (0.67)
  Pallas kernels: 27.8 us -> 10.8 us
  local copies, waits for them, and re-layouts: 4.28 us -> 2.29 us
    pallas_call x1, Pallas kernels: 12 us -> 4.83 us  [body(): pl.pallas_call(main_kernel, grid=(1,), out_shape=jax.ShapeDtypeStruct((WI...]
    pallas_call x1, Pallas kernels: 9.17 us -> 2.14 us  [body(): pl.pallas_call(tail_kernel, grid=(1,), out_shape=jax.ShapeDtypeStruct((WI...]
    pallas_call x1, Pallas kernels: 3.22 us -> 1.24 us  [body(): pl.pallas_call(functools.partial(sort_kernel, capacity=capacity), out_sha...]
    broadcast_in_dim x2 -> x0, local copies, waits for them, and re-layouts: 1.47 us -> none  [the longest x1 0.74 us: body(): jnp.broadcast_to(score_weight.astype(jnp.float32)[:, None], (hidden, CHUNK))]
    pallas_call x1, Pallas kernels: 3.4 us -> 2.44 us  [body(): pl.pallas_call(functools.partial(pack_kernel, devices=devices, capacity=c...]
    unnamed x11 -> x10, local copies, waits for them, and re-layouts: 2.81 us -> 2.29 us
  transfers between devices with their start and end apart: 2 -> 2, of which waited for: 1 -> 1; matrix products, arithmetic and copies ran while one was open for 4% -> 0% of each run, Pallas kernels for 21% -> 13%
where the time goes in v2:
time: 38.7 us; the launch traced here: 38.4 us
  waiting for transfers between devices  15.7 us (41%)
  Pallas kernels  10.8 us (28%)
  starting transfers between devices  9.51 us (25%)
  local copies, waits for them, and re-layouts  2.29 us (6%)
    all_to_all x1, waiting for transfers between devices, body(): lax.all_to_all(outgoing, 'dev', split_axis=0, concat_axis=0, tiled=True)  15.7 us
    all_to_all x1, starting transfers between devices, body(): lax.all_to_all(outgoing, 'dev', split_axis=0, concat_axis=0, tiled=True)  7.08 us
    pallas_call x1, Pallas kernels, body(): pl.pallas_call(main_kernel, grid=(1,), out_shape=jax.ShapeDtypeStruct((WI...  4.83 us
    pallas_call x1, Pallas kernels, body(): pl.pallas_call(functools.partial(pack_kernel, devices=devices, capacity=c...  2.44 us
    ppermute x1, starting transfers between devices, body(): lax.ppermute(head, 'dev', [(i, i - 1) for i in range(1, devices)])  2.43 us
    unnamed x10, local copies, waits for them, and re-layouts  2.29 us
    pallas_call x1, Pallas kernels, body(): pl.pallas_call(tail_kernel, grid=(1,), out_shape=jax.ShapeDtypeStruct((WI...  2.14 us
    pallas_call x1, Pallas kernels, body(): pl.pallas_call(functools.partial(sort_kernel, capacity=capacity), out_sha...  1.24 us
  transfers between devices with their start and end apart: 2, of which 1 were waited for; matrix products, arithmetic and copies ran while one was open for 0% of the time, Pallas kernels for 13%

profile of v2, /device:TPU:1, one launch (start us, length us, event | category | flops | bytes accessed | tf_op | source)
XLA Modules:
  0.0 38.4 jit_solution(11679859277679614410)
XLA Ops:
  0.0 0.0 copy-start
  0.0 0.9 %copy-done = bf16[1024,128]{1,0:T(8,128)(2,1)S(1)} copy-done((bf16[1024,128]{1,0:T(8,128)(2,1)S(1)}, bf16[1024,128]{1,0:T(8,128)(2,1)}, u32[]{:S(2)}) %copy-start) | copy-done | bytes 262168
  1.0 0.0 copy-start.2
  1.0 0.7 %copy-done.2 = s32[1024]{0:T(1024)S(1)} copy-done((s32[1024]{0:T(1024)S(1)}, s32[1024]{0:T(1024)}, u32[]{:S(2)}) %copy-start.2) | copy-done | bytes 4120
  1.6 2.4 %pack.1 = bf16[32,72,128]{2,1,0:T(8,128)(2,1)} custom-call(s32[1,1024]{1,0:T(1,128)S(1)} %bitcast.4, bf16[1024,128]{1,0:T(8,128)(2,1)S(1)} %copy-done), custom_call_target="tpu_custom_call" | custom-call | tf_op jit(solution)/shard_map/pack/pallas_call | solution.py:170
  4.1 0.0 copy-start.1
  4.1 7.1 %all-to-all-start = ((bf16[32,72,128]{2,1,0:T(8,128)(2,1)}), bf16[32,72,128]{2,1,0:T(8,128)(2,1)S(1)}, u32[]{:S(2)}, u32[]{:S(2)}) async-start(bf16[32,72,128]{2,1,0:T(8,128)(2,1)} %pack.1), calls=%async_computation | async-start | bytes 1179648 | tf_op jit(solution)/shard_map/all_to_all | solution.py:178
  11.2 0.0 copy-start.3
  11.2 0.0 copy-start.4
  11.2 0.0 copy-done.1
  11.2 0.6 %copy-done.3 = f32[128]{0:T(128)S(1)} copy-done((f32[128]{0:T(128)S(1)}, f32[128]{0:T(128)}, u32[]{:S(2)}) %copy-start.3) | copy-done | bytes 536
  11.8 0.0 copy-done.4
  11.9 0.1 prepare.1
  12.0 15.7 %all-to-all-done.arrived_ref = bf16[32,72,128]{2,1,0:T(8,128)(2,1)S(1)} async-done(((bf16[32,72,128]{2,1,0:T(8,128)(2,1)}), bf16[32,72,128]{2,1,0:T(8,128)(2,1)S(1)}, u32[]{:S(2)}, u32[]{:S(2)}) %all-to-all-start) | async-done | bytes 589856 | tf_op jit(solution)/shard_map/all_to_all | solution.py:178
  27.7 1.2 %sort.1 = (f32[1024,128]{1,0:T(8,128)S(1)}, bf16[32,128]{1,0:T(8,128)(2,1)S(1)}) custom-call(bf16[32,72,128]{2,1,0:T(8,128)(2,1)S(1)} %all-to-all-done.arrived_ref, bf16[128,256]{1,0:T(8,128)(2,1)S(1)} %get-tuple-element.11.refs_0_.turned_ref, f32[128,256]{1,0:T(8,128)S(1)} %get-tuple-element.12.refs_1_.floor_ref, ...), custom_call_target="tpu_custom_call" | custom-call | tf_op jit(solution)/shard_map/sort/pallas_call | solution.py:193
  29.0 2.4 %collective-permute-start = (bf16[32,128]{1,0:T(8,128)(2,1)S(1)}, bf16[32,128]{1,0:T(8,128)(2,1)S(1)}, u32[]{:S(2)}, u32[]{:S(2)}) collective-permute-start(bf16[32,128]{1,0:T(8,128)(2,1)S(1)} %get-tuple-element.16), channel_id=1, source_target_pairs={{1,0},{2,1},{3,2},{4,3},{5,4},{6,5},{7,6},{8,7},{9,8},{10,9},{11,1... | collective-permute-start | bytes 24584 | tf_op jit(solution)/shard_map/ppermute | solution.py:204
  31.4 4.8 %main.1._ = f32[31,1024]{1,0:T(8,128)} custom-call(f32[1024,128]{1,0:T(8,128)S(1)} %get-tuple-element.15.wide_ref, bf16[128,256]{1,0:T(8,128)(2,1)S(1)} %get-tuple-element.11.refs_0_.turned_ref, f32[128,256]{1,0:T(8,128)S(1)} %get-tuple-element.12.refs_1_.floor_ref, f32[128,256]{1,0:T(8,128)S(1)} %get-tuple-element.13.refs_2_.scale_ref, ...), custom_call_target="tpu_custom_call" | custom-call | flops 1560281088 | bytes 95232 | tf_op jit(solution)/shard_map/main/pallas_call | solution.py:207
  36.2 0.0 collective-permute-done.next_ref
  36.2 2.1 %tail.1 = f32[31,1024]{1,0:T(8,128)} custom-call(s32[1]{0:T(128)} %bitcast.limit_ref, f32[1024,128]{1,0:T(8,128)S(1)} %get-tuple-element.15.wide_ref, bf16[32,128]{1,0:T(8,128)(2,1)S(1)} %collective-permute-done.next_ref, bf16[128,256]{1,0:T(8,128)(2,1)S(1)} %get-tuple-element.11.refs_0_.turned_ref, ...), custom_call_target="tpu_custom_call", output_to_operand_aliasing={{}: (7, {})} | custom-call | tf_op jit(solution)/shard_map/tail/pallas_call | solution.py:221
Async XLA Ops:
  0.0 0.9 %copy-start = (bf16[1024,128]{1,0:T(8,128)(2,1)S(1)}, bf16[1024,128]{1,0:T(8,128)(2,1)}, u32[]{:S(2)}) copy-start(bf16[1024,128]{1,0:T(8,128)(2,1)} %rows_ref.1) | copy-start | bytes 786436
  1.0 0.7 %copy-start.2 = (s32[1024]{0:T(1024)S(1)}, s32[1024]{0:T(1024)}, u32[]{:S(2)}) copy-start(s32[1024]{0:T(1024)} %param.6) | copy-start | bytes 12292
  4.1 7.1 %copy-start.1 = (bf16[256,128]{1,0:T(8,128)(2,1)S(1)}, bf16[256,128]{1,0:T(8,128)(2,1)}, u32[]{:S(2)}) copy-start(bf16[256,128]{1,0:T(8,128)(2,1)} %weight_ref.1) | copy-start | bytes 196612
  4.1 23.6 %all-to-all-start = ((bf16[32,72,128]{2,1,0:T(8,128)(2,1)}), bf16[32,72,128]{2,1,0:T(8,128)(2,1)S(1)}, u32[]{:S(2)}, u32[]{:S(2)}) async-start(bf16[32,72,128]{2,1,0:T(8,128)(2,1)} %pack.1), calls=%async_computation | async-start | bytes 1179648 | tf_op jit(solution)/shard_map/all_to_all | solution.py:178
  11.2 0.7 %copy-start.3 = (f32[128]{0:T(128)S(1)}, f32[128]{0:T(128)}, u32[]{:S(2)}) copy-start(f32[128]{0:T(128)} %param.8) | copy-start | bytes 1540
  11.2 0.7 %copy-start.4 = (bf16[128]{0:T(256)(128)(2,1)S(1)}, bf16[128]{0:T(256)(128)(2,1)}, u32[]{:S(2)}) copy-start(bf16[128]{0:T(256)(128)(2,1)} %param.9) | copy-start | bytes 772
  29.0 7.3 %collective-permute-start = (bf16[32,128]{1,0:T(8,128)(2,1)S(1)}, bf16[32,128]{1,0:T(8,128)(2,1)S(1)}, u32[]{:S(2)}, u32[]{:S(2)}) collective-permute-start(bf16[32,128]{1,0:T(8,128)(2,1)S(1)} %get-tuple-element.16), channel_id=1, source_target_pairs={{1,0},{2,1},{3,2},{4,3},{5,4},{6,5},{7,6},{8,7},{9,8},{10,9},{11,1... | collective-permute-start | bytes 24584 | tf_op jit(solution)/shard_map/ppermute | solution.py:204

commit v3 on v2

--- a/solution.py
+++ b/solution.py
@@ -27,8 +27,13 @@
     return jnp.where((local >= 0) & (local < CHUNK), local, -1)
 
 
-def pack_kernel(ranks_ref, rows_ref, out_ref, *, devices, capacity):
+def pack_kernel(ranks_hbm, rows_hbm, out_ref, ranks_ref, rows_ref, sems, *, devices, capacity):
+    ranks_copy = pltpu.make_async_copy(ranks_hbm, ranks_ref, sems.at[0])
+    rows_copy = pltpu.make_async_copy(rows_hbm, rows_ref, sems.at[1])
+    ranks_copy.start()
+    rows_copy.start()
     count = rows_ref.shape[0]
+    ranks_copy.wait()
     ranks = ranks_ref[...]
     owner = ranks // count
     position = ranks - owner * count
@@ -53,6 +58,7 @@
     slot = jnp.concatenate(slots, axis=1)
     target = owner * capacity + slot.astype(jnp.int32)
 
+    rows_copy.wait()
     rows = rows_ref[...]
     group = CHUNK // capacity
     for chunk in range(devices * capacity // CHUNK):
@@ -74,8 +80,7 @@
     out_ref[:, capacity:, :] = places.reshape(devices, 8, LANES).astype(jnp.bfloat16)
 
 
-def sort_kernel(arrived_ref, *refs, capacity):
-    wide_ref, head_ref = refs[-2:]
+def ordered_chunks(arrived_ref, count, capacity):
     devices = arrived_ref.shape[0]
     share = LANES // capacity
     lane = lax.broadcasted_iota(jnp.int32, (8, LANES), 1)
@@ -90,12 +95,9 @@
     high = jnp.concatenate(highs, axis=1)
     low = jnp.concatenate(lows, axis=1)
     rows = arrived_ref[:, :capacity, :].reshape(devices * capacity, LANES)
-    for chunk in range(wide_ref.shape[0] // CHUNK):
+    for chunk in range(count // CHUNK):
         pick = one_hot(jnp.where(high == chunk + 1, low, -1.0), CHUNK)
-        ordered = jnp.dot(pick, rows, preferred_element_type=jnp.float32)
-        wide_ref[chunk * CHUNK : (chunk + 1) * CHUNK, :] = ordered
-        if chunk == 0:
-            head_ref[...] = ordered[:WIN].astype(jnp.bfloat16)
+        yield jnp.dot(pick, rows, preferred_element_type=jnp.float32)
 
 
 def prepare_kernel(weight_ref, bias_ref, score_ref, turned_ref, floor_ref, scale_ref, base_ref):
@@ -111,54 +113,72 @@
     )
 
 
-def score_tile(leading, partner, weight, floor_ref, scale_ref, base_ref):
-    features = jnp.concatenate([leading * partner, jnp.abs(leading - partner)], axis=1)
-    hidden = lax.dot_general(
-        weight, features, (((1,), (1,)), ((), ())), preferred_element_type=jnp.float32
-    )
-    hidden = jnp.maximum(hidden, floor_ref[...]) * scale_ref[...]
-    return jnp.sum(hidden, axis=0, keepdims=True) + base_ref[...]
-
-
-def score_blocks(blocks, wide_ref, write, parameters):
-    weight = parameters[0][...]
-    half = WIN // 2
-    leadings = [wide_ref[b * CHUNK : (b + 1) * CHUNK, :].astype(jnp.bfloat16) for b in range(blocks)]
-    for offset in range(1, half + 1):
-        for b in range(blocks):
-            first = b * CHUNK + offset
-            extra = half if offset < half else 0
-            partner = wide_ref[first : first + CHUNK + extra, :].astype(jnp.bfloat16)
-            for add in (0, half)[: 2 if extra else 1]:
-                line = score_tile(
-                    leadings[b], partner[add : add + CHUNK], weight, *parameters[1:]
-                )
-                write(offset + add, b, line)
-
-
-def main_kernel(wide_ref, turned_ref, floor_ref, scale_ref, base_ref, out_ref):
-    def write(offset, block, line):
-        out_ref[offset - 1 : offset, block * CHUNK : (block + 1) * CHUNK] = line
-
-    score_blocks(
-        out_ref.shape[1] // CHUNK, wide_ref, write, (turned_ref, floor_ref, scale_ref, base_ref)
-    )
+def score_block(columns, write, turned_ref, floor_ref, scale_ref, base_ref):
+    columns = columns.astype(jnp.bfloat16)
+    leading = columns[:, :CHUNK]
+    weight = turned_ref[...]
+    for offset in range(1, WIN):
+        partner = pltpu.roll(columns, columns.shape[1] - offset, 1)[:, :CHUNK]
+        features = jnp.concatenate(
+            [leading * partner, jnp.abs(leading - partner)], axis=0
+        )
+        hidden = jnp.dot(weight, features, preferred_element_type=jnp.float32)
+        hidden = jnp.maximum(hidden, floor_ref[...]) * scale_ref[...]
+        write(offset, jnp.sum(hidden, axis=0, keepdims=True) + base_ref[...])
+
+
+def score_inner(wide_ref, out_ref, first, parameters):
+    for block in range(out_ref.shape[1] // CHUNK):
+        start = (first + block) * CHUNK
+
+        def write(offset, line, place=block * CHUNK):
+            out_ref[offset - 1 : offset, place : place + CHUNK] = line
+
+        score_block(wide_ref[:, start : start + CHUNK + LANES], write, *parameters)
+
+
+def sort_kernel(arrived_ref, *refs, capacity):
+    parameters, (wide_ref, head_ref, out_ref) = refs[:4], refs[4:]
+    for chunk, ordered in enumerate(ordered_chunks(arrived_ref, wide_ref.shape[1], capacity)):
+        wide_ref[:, chunk * CHUNK : (chunk + 1) * CHUNK] = ordered.T
+        if chunk == 0:
+            head_ref[...] = ordered[: head_ref.shape[0]].astype(jnp.bfloat16)
+    score_inner(wide_ref, out_ref, 0, parameters)
+
+
+def middle_kernel(wide_ref, *refs, first):
+    score_inner(wide_ref, refs[4], first, refs[:4])
 
 
 def tail_kernel(
-    limit_ref, wide_ref, next_ref, turned_ref, floor_ref, scale_ref, base_ref, _, out_ref,
-    joined_ref,
+    limit_ref, wide_ref, next_ref, turned_ref, floor_ref, scale_ref, base_ref,
+    early_ref, middle_ref, out_ref, late_ref, sems,
 ):
-    count = wide_ref.shape[0]
-    joined_ref[:CHUNK, :] = wide_ref[count - CHUNK :, :]
-    joined_ref[CHUNK:, :] = next_ref[...].astype(jnp.float32)
-    place = count - CHUNK + lax.broadcasted_iota(jnp.int32, (1, CHUNK), 1)
+    count = wide_ref.shape[1]
+    base = count - CHUNK
+    split = early_ref.shape[1]
+    copies = [
+        pltpu.make_async_copy(early_ref, out_ref.at[:, :split], sems.at[0]),
+        pltpu.make_async_copy(middle_ref, out_ref.at[:, split:base], sems.at[1]),
+    ]
+    for copy in copies:
+        copy.start()
+    following = next_ref[...].astype(jnp.float32)
+    padding = jnp.zeros((LANES - following.shape[0], LANES), jnp.float32)
+    following = jnp.concatenate([following, padding], axis=0).T
+    columns = jnp.concatenate([wide_ref[:, base:], following], axis=1)
+    place = base + lax.broadcasted_iota(jnp.int32, (1, CHUNK), 1)
     limit = limit_ref[0]
 
-    def write(offset, block, line):
-        out_ref[offset - 1 : offset, :] = jnp.where(place + offset < limit, line, 0.0)
-
-    score_blocks(1, joined_ref, write, (turned_ref, floor_ref, scale_ref, base_ref))
+    def write(offset, line):
+        late_ref[offset - 1 : offset, :] = jnp.where(place + offset < limit, line, 0.0)
+
+    score_block(columns, write, turned_ref, floor_ref, scale_ref, base_ref)
+    last = pltpu.make_async_copy(late_ref, out_ref.at[:, base:], sems.at[2])
+    last.start()
+    for copy in copies:
+        copy.wait()
+    last.wait()
 
 
 def body(embeddings, ranks, pair_weight, pair_bias, score_weight):
@@ -170,9 +190,13 @@
     outgoing = pl.pallas_call(
         functools.partial(pack_kernel, devices=devices, capacity=capacity),
         out_shape=jax.ShapeDtypeStruct((devices, capacity + 8, width), jnp.bfloat16),
-        in_specs=[VMEM] * 2,
+        in_specs=[ANY] * 2,
         out_specs=VMEM,
-        compiler_params=SMALL,
+        scratch_shapes=[
+            pltpu.VMEM((1, rows_dev), jnp.int32),
+            pltpu.VMEM((rows_dev, width), jnp.bfloat16),
+            pltpu.SemaphoreType.DMA((2,)),
+        ],
         name="pack",
     )(ranks.reshape(1, rows_dev), embeddings)
     arrived = lax.all_to_all(outgoing, "dev", split_axis=0, concat_axis=0, tiled=True)
@@ -190,45 +214,52 @@
         name="prepare",
     )(pair_weight, pair_bias.reshape(1, hidden), score_weight.reshape(1, hidden))
 
-    wide, head = pl.pallas_call(
+    def cost(columns):
+        pairs = (WIN - 1) * columns
+        return pl.CostEstimate(
+            flops=4 * pairs * width * hidden, bytes_accessed=4 * pairs, transcendentals=0
+        )
+
+    early = CHUNK
+    middle = rows_dev - 2 * CHUNK
+    wide, head, scores_early = pl.pallas_call(
         functools.partial(sort_kernel, capacity=capacity),
         out_shape=(
-            jax.ShapeDtypeStruct((rows_dev, width), jnp.float32),
+            jax.ShapeDtypeStruct((width, rows_dev), jnp.float32),
             jax.ShapeDtypeStruct((WIN, width), jnp.bfloat16),
+            jax.ShapeDtypeStruct((WIN - 1, early), jnp.float32),
         ),
-        in_specs=[VMEM] + [ANY] * 4,
-        out_specs=(VMEM, VMEM),
+        in_specs=[VMEM] * 5,
+        out_specs=(VMEM,) * 3,
+        cost_estimate=cost(early),
         compiler_params=SMALL,
         name="sort",
     )(arrived, *parameters)
     following = lax.ppermute(head, "dev", [(i, i - 1) for i in range(1, devices)])
-
-    pairs = (WIN - 1) * (rows_dev - CHUNK)
-    scores = pl.pallas_call(
-        main_kernel,
-        grid=(1,),
-        out_shape=jax.ShapeDtypeStruct((WIN - 1, rows_dev), jnp.float32),
+    scores_middle = pl.pallas_call(
+        functools.partial(middle_kernel, first=early // CHUNK),
+        out_shape=jax.ShapeDtypeStruct((WIN - 1, middle), jnp.float32),
         in_specs=[VMEM] * 5,
-        out_specs=pl.BlockSpec((WIN - 1, rows_dev - CHUNK), lambda i: (0, 0)),
-        cost_estimate=pl.CostEstimate(
-            flops=4 * pairs * width * hidden, bytes_accessed=4 * pairs, transcendentals=0
-        ),
-        compiler_params=SMALL,
-        name="main",
+        out_specs=VMEM,
+        cost_estimate=cost(middle),
+        compiler_params=SMALL,
+        name="middle",
     )(wide, *parameters)
     last = lax.axis_index("dev") == devices - 1
     limit = jnp.where(last, rows_dev, 2 * rows_dev).astype(jnp.int32).reshape(1)
     return pl.pallas_call(
         tail_kernel,
-        grid=(1,),
         out_shape=jax.ShapeDtypeStruct((WIN - 1, rows_dev), jnp.float32),
-        in_specs=[SMEM] + [VMEM] * 6 + [ANY],
-        out_specs=pl.BlockSpec((WIN - 1, CHUNK), lambda i: (0, rows_dev // CHUNK - 1)),
-        scratch_shapes=[pltpu.VMEM((CHUNK + WIN, width), jnp.float32)],
-        input_output_aliases={7: 0},
+        in_specs=[SMEM] + [VMEM] * 8,
+        out_specs=ANY,
+        scratch_shapes=[
+            pltpu.VMEM((WIN - 1, CHUNK), jnp.float32),
+            pltpu.SemaphoreType.DMA((3,)),
+        ],
+        cost_estimate=cost(CHUNK),
         compiler_params=SMALL,
         name="tail",
-    )(limit, wide, following, *parameters, scores)
+    )(limit, wide, following, *parameters, scores_early, scores_middle)
 
 
 def solution(mesh):

time: 38.7 us -> 36.2 us (0.935)
  local copies, waits for them, and re-layouts: 2.29 us -> 0.65 us
  Pallas kernels: 10.8 us -> 9.57 us
    pallas_call x2, Pallas kernels: 6.97 us -> 4.23 us  [the longest x1 2.23 us: body(): pl.pallas_call(functools.partial(middle_kernel, first=early // CHUNK), ou...]
    unnamed x10 -> x6, local copies, waits for them, and re-layouts: 2.29 us -> 0.65 us
    pallas_call x1, Pallas kernels: 1.24 us -> 2.01 us  [body(): pl.pallas_call(functools.partial(sort_kernel, capacity=capacity), out_sha...]
    pallas_call x1, Pallas kernels: 2.44 us -> 3.2 us  [body(): pl.pallas_call(functools.partial(pack_kernel, devices=devices, capacity=c...]
  transfers between devices with their start and end apart: 2 -> 2, of which waited for: 1 -> 2; matrix products, arithmetic and copies ran while one was open for 0% -> 0% of each run, Pallas kernels for 13% -> 7%
where the time goes in v3:
time: 36.2 us; the launch traced here: 35.8 us
  waiting for transfers between devices  16 us (44%)
  Pallas kernels  9.57 us (26%)
  starting transfers between devices  9.53 us (26%)
  local copies, waits for them, and re-layouts  0.65 us (2%)
    all_to_all x1, waiting for transfers between devices, body(): lax.all_to_all(outgoing, 'dev', split_axis=0, concat_axis=0, tiled=True)  15.7 us
    all_to_all x1, starting transfers between devices, body(): lax.all_to_all(outgoing, 'dev', split_axis=0, concat_axis=0, tiled=True)  7.09 us
    pallas_call x1, Pallas kernels, body(): pl.pallas_call(functools.partial(pack_kernel, devices=devices, capacity=c...  3.2 us
    ppermute x1, starting transfers between devices, body(): lax.ppermute(head, 'dev', [(i, i - 1) for i in range(1, devices)])  2.43 us
    pallas_call x1, Pallas kernels, body(): pl.pallas_call(functools.partial(middle_kernel, first=early // CHUNK), ou...  2.23 us
    pallas_call x1, Pallas kernels, body(): pl.pallas_call(functools.partial(sort_kernel, capacity=capacity), out_sha...  2.01 us
    pallas_call x1, Pallas kernels, body(): pl.pallas_call(tail_kernel, out_shape=jax.ShapeDtypeStruct((WIN - 1, rows...  2 us
  transfers between devices with their start and end apart: 2, of which 2 were waited for; matrix products, arithmetic and copies ran while one was open for 0% of the time, Pallas kernels for 7%

profile of v3, /device:TPU:1, one launch (start us, length us, event | category | flops | bytes accessed | tf_op | source)
XLA Modules:
  0.0 35.8 jit_solution(3560985826845746899)
XLA Ops:
  0.0 3.2 %pack.1 = bf16[32,72,128]{2,1,0:T(8,128)(2,1)} custom-call(s32[1,1024]{1,0:T(1,128)} %bitcast.6, bf16[1024,128]{1,0:T(8,128)(2,1)} %rows_hbm.1), custom_call_target="tpu_custom_call" | custom-call | tf_op jit(solution)/shard_map/pack/pallas_call | solution.py:190
  3.2 0.0 copy-start
  3.2 7.1 %all-to-all-start = ((bf16[32,72,128]{2,1,0:T(8,128)(2,1)}), bf16[32,72,128]{2,1,0:T(8,128)(2,1)S(1)}, u32[]{:S(2)}, u32[]{:S(2)}) async-start(bf16[32,72,128]{2,1,0:T(8,128)(2,1)} %pack.1), calls=%async_computation | async-start | bytes 1179648 | tf_op jit(solution)/shard_map/all_to_all | solution.py:202
  10.3 0.0 copy-start.1
  10.3 0.0 copy-start.2
  10.4 0.0 copy-done
  10.4 0.6 %copy-done.1 = f32[128]{0:T(128)S(1)} copy-done((f32[128]{0:T(128)S(1)}, f32[128]{0:T(128)}, u32[]{:S(2)}) %copy-start.1) | copy-done | bytes 536
  11.0 0.0 copy-done.2
  11.0 0.1 prepare.1
  11.1 15.7 %all-to-all-done.arrived_ref = bf16[32,72,128]{2,1,0:T(8,128)(2,1)S(1)} async-done(((bf16[32,72,128]{2,1,0:T(8,128)(2,1)}), bf16[32,72,128]{2,1,0:T(8,128)(2,1)S(1)}, u32[]{:S(2)}, u32[]{:S(2)}) %all-to-all-start) | async-done | bytes 589856 | tf_op jit(solution)/shard_map/all_to_all | solution.py:202
  26.9 2.0 %sort.1 = (f32[128,1024]{1,0:T(8,128)S(1)}, bf16[32,128]{1,0:T(8,128)(2,1)S(1)}, f32[31,256]{1,0:T(8,128)S(1)}) custom-call(bf16[32,72,128]{2,1,0:T(8,128)(2,1)S(1)} %all-to-all-done.arrived_ref, bf16[128,256]{1,0:T(8,128)(2,1)S(1)} %get-tuple-element.12.refs_0_.turned_ref, f32[128,256]{1,0:T(8,128)S(1)} %get-tuple-element.13.refs_1_.floor_ref, ...), custom_call_target="tpu_custom_call" | custom-call | flops 520093696 | bytes 31744 | tf_op jit(solution)/shard_map/sort/pallas_call | solution.py:225
  28.9 2.4 %collective-permute-start = (bf16[32,128]{1,0:T(8,128)(2,1)S(1)}, bf16[32,128]{1,0:T(8,128)(2,1)S(1)}, u32[]{:S(2)}, u32[]{:S(2)}) collective-permute-start(bf16[32,128]{1,0:T(8,128)(2,1)S(1)} %get-tuple-element.17), channel_id=1, source_target_pairs={{1,0},{2,1},{3,2},{4,3},{5,4},{6,5},{7,6},{8,7},{9,8},{10,9},{11,1... | collective-permute-start | bytes 24584 | tf_op jit(solution)/shard_map/ppermute | solution.py:238
  31.3 2.2 %middle.1.middle_ref = f32[31,512]{1,0:T(8,128)S(1)} custom-call(f32[128,1024]{1,0:T(8,128)S(1)} %get-tuple-element.16.wide_ref, bf16[128,256]{1,0:T(8,128)(2,1)S(1)} %get-tuple-element.12.refs_0_.turned_ref, f32[128,256]{1,0:T(8,128)S(1)} %get-tuple-element.13.refs_1_.floor_ref, f32[128,256]{1,0:T(8,128)S(1)} %get-tuple-element.14.refs_2_.scale_ref, ...), custom_call_target="tpu_custom_call" | custom-call | flops 1040187392 | bytes 63488 | tf_op jit(solution)/shard_map/middle/pallas_call | solution.py:239
  33.6 0.3 collective-permute-done.next_ref
  33.8 2.0 %tail.1 = f32[31,1024]{1,0:T(8,128)} custom-call(s32[1]{0:T(128)} %bitcast.limit_ref, f32[128,1024]{1,0:T(8,128)S(1)} %get-tuple-element.16.wide_ref, bf16[32,128]{1,0:T(8,128)(2,1)S(1)} %collective-permute-done.next_ref, bf16[128,256]{1,0:T(8,128)(2,1)S(1)} %get-tuple-element.12.refs_0_.turned_ref, f32[128,256]{1,0:T(8,128)S(1)} %get-tuple-element.13.refs_1_.floor_ref, ...), custom_call_target="tpu_custom_call" | custom-call | flops 520093696 | bytes 31744 | tf_op jit(solution)/shard_map/tail/pallas_call | solution.py:250
Async XLA Ops:
  3.2 7.1 %copy-start = (bf16[256,128]{1,0:T(8,128)(2,1)S(1)}, bf16[256,128]{1,0:T(8,128)(2,1)}, u32[]{:S(2)}) copy-start(bf16[256,128]{1,0:T(8,128)(2,1)} %weight_ref.1) | copy-start | bytes 196612
  3.2 23.6 %all-to-all-start = ((bf16[32,72,128]{2,1,0:T(8,128)(2,1)}), bf16[32,72,128]{2,1,0:T(8,128)(2,1)S(1)}, u32[]{:S(2)}, u32[]{:S(2)}) async-start(bf16[32,72,128]{2,1,0:T(8,128)(2,1)} %pack.1), calls=%async_computation | async-start | bytes 1179648 | tf_op jit(solution)/shard_map/all_to_all | solution.py:202
  10.3 0.7 %copy-start.1 = (f32[128]{0:T(128)S(1)}, f32[128]{0:T(128)}, u32[]{:S(2)}) copy-start(f32[128]{0:T(128)} %param.8) | copy-start | bytes 1540
  10.3 0.7 %copy-start.2 = (bf16[128]{0:T(256)(128)(2,1)S(1)}, bf16[128]{0:T(256)(128)(2,1)}, u32[]{:S(2)}) copy-start(bf16[128]{0:T(256)(128)(2,1)} %param.9) | copy-start | bytes 772
  28.9 5.0 %collective-permute-start = (bf16[32,128]{1,0:T(8,128)(2,1)S(1)}, bf16[32,128]{1,0:T(8,128)(2,1)S(1)}, u32[]{:S(2)}, u32[]{:S(2)}) collective-permute-start(bf16[32,128]{1,0:T(8,128)(2,1)S(1)} %get-tuple-element.17), channel_id=1, source_target_pairs={{1,0},{2,1},{3,2},{4,3},{5,4},{6,5},{7,6},{8,7},{9,8},{10,9},{11,1... | collective-permute-start | bytes 24584 | tf_op jit(solution)/shard_map/ppermute | solution.py:238

commit v4 on v3

v4 whole, which is shorter than its diff:
```python
import functools

import jax
import jax.numpy as jnp
from jax import lax
from jax.experimental import pallas as pl
from jax.experimental.pallas import tpu as pltpu
from jax.sharding import PartitionSpec as P

WIN = 32
LANES = 128
CHUNK = 256
SPARE = 6
LOST = 255.0
VMEM = pl.BlockSpec(memory_space=pltpu.VMEM)
SMEM = pl.BlockSpec(memory_space=pltpu.SMEM)
ANY = pl.BlockSpec(memory_space=pl.ANY)
HBM = pl.BlockSpec(memory_space=pltpu.HBM)
SMALL = pltpu.CompilerParams(vmem_limit_bytes=16 * 2**20)


def matches(values, count):
    index = lax.broadcasted_iota(jnp.int32, (count, 1), 0).astype(jnp.float32)
    return values.astype(jnp.bfloat16) == index.astype(jnp.bfloat16)


def one_hot(values, count):
    return jnp.where(matches(values, count), jnp.bfloat16(1), jnp.bfloat16(0))


def in_chunk(values, chunk):
    local = values - chunk * CHUNK
    return jnp.where((local >= 0) & (local < CHUNK), local, -1)


def pack_kernel(
    me_ref, ranks_hbm, rows_hbm, out_ref, ranks_ref, rows_ref, sems, *, devices, capacity
):
    ranks_copy = pltpu.make_async_copy(ranks_hbm, ranks_ref, sems.at[0])
    rows_copy = pltpu.make_async_copy(rows_hbm, rows_ref, sems.at[1])
    ranks_copy.start()
    rows_copy.start()
    count = rows_ref.shape[0]
    ranks_copy.wait()
    ranks = ranks_ref[...]
    owner = ranks // count
    position = ranks - owner * count
    before_owner = jnp.where(position < WIN - 1, owner, 0) - 1

    device_ids = lax.broadcasted_iota(jnp.int32, (devices, 1), 0)
    before = (
        lax.broadcasted_iota(jnp.int32, (CHUNK, CHUNK), 0)
        < lax.broadcasted_iota(jnp.int32, (CHUNK, CHUNK), 1)
    )
    before = jnp.where(before, 1.0, 0.0).astype(jnp.bfloat16)
    totals = jnp.zeros((2 * devices, 1), jnp.float32)
    members, indices = [], []
    for start in range(0, count, CHUNK):
        span = slice(start, start + CHUNK)
        member = jnp.concatenate(
            [
                jnp.where(device_ids == owner[:, span], 1.0, 0.0),
                jnp.where(device_ids == before_owner[:, span], 1.0, 0.0),
            ],
            axis=0,
        )
        earlier = jnp.dot(
            member.astype(jnp.bfloat16), before, preferred_element_type=jnp.float32
        )
        members.append(member)
        indices.append(earlier + totals)
        totals = totals + jnp.sum(member, axis=1, keepdims=True)
    owned = totals[:devices]
    slot = jnp.concatenate(
        [
            jnp.sum(m[:devices] * i[:devices], axis=0, keepdims=True)
            for m, i in zip(members, indices)
        ],
        axis=1,
    ).astype(jnp.int32)
    again = jnp.concatenate(
        [
            jnp.sum(m[devices:] * (i[devices:] + owned), axis=0, keepdims=True)
            for m, i in zip(members, indices)
        ],
        axis=1,
    ).astype(jnp.int32)
    extra = before_owner >= 0
    fits = extra & (again < capacity)
    spare = extra & (again >= capacity) & (again < capacity + SPARE)
    lost = jnp.where(extra & (again >= capacity + SPARE), 1.0, 0.0)
    target = owner * capacity + slot
    second = jnp.where(fits, before_owner * capacity + again, -1)
    third = jnp.where(spare, before_owner * 8 + (again - capacity + 8 - SPARE), -1)

    high = (position // CHUNK + 1).astype(jnp.float32)
    low = (position % CHUNK).astype(jnp.float32)
    head = position.astype(jnp.float32)
    lane = lax.broadcasted_iota(jnp.int32, (LANES, 1), 0)
    corner = (me_ref[0] % (LANES // 8)) * 8
    spot = jnp.where(slot == lane % capacity, 1.0, 0.0).astype(jnp.bfloat16)
    where_again = jnp.where(
        fits, again, jnp.where(spare, LANES + corner + again - capacity + 8 - SPARE, -1)
    )
    spot_again = jnp.where(
        (where_again == lane % capacity) | (where_again == LANES + lane), 1.0, 0.0
    ).astype(jnp.bfloat16)
    mine = device_ids == owner
    theirs = device_ids == before_owner
    values = jnp.concatenate(
        [
            jnp.where(mine, high, 0.0),
            jnp.where(mine, low, 0.0),
            jnp.zeros((devices, count), jnp.float32),
        ],
        axis=0,
    ).astype(jnp.bfloat16)
    values_again = jnp.concatenate(
        [
            jnp.where(theirs & fits, jnp.float32(count // CHUNK + 1), 0.0),
            jnp.where(theirs & fits, head, 0.0),
            jnp.where(theirs & spare, head + 1.0, 0.0),
        ],
        axis=0,
    ).astype(jnp.bfloat16)
    contract = (((1,), (1,)), ((), ()))
    places = lax.dot_general(
        values, spot, contract, preferred_element_type=jnp.float32
    ) + lax.dot_general(
        values_again, spot_again, contract, preferred_element_type=jnp.float32
    )
    lane_row = lax.broadcasted_iota(jnp.int32, (1, LANES), 1)
    main_line = jnp.where(
        lane_row < capacity, places[:devices], places[devices : 2 * devices]
    )
    lost = jnp.max(lost, axis=1, keepdims=True)
    spare_line = places[2 * devices :] + jnp.where(lane_row == corner, LOST * lost, 0.0)

    rows_copy.wait()
    rows = rows_ref[...]
    group = CHUNK // capacity
    for chunk in range(devices * capacity // CHUNK):
        pick = jnp.where(
            matches(in_chunk(target, chunk), CHUNK) | matches(in_chunk(second, chunk), CHUNK),
            jnp.bfloat16(1),
            jnp.bfloat16(0),
        )
        packed = jnp.dot(pick, rows, preferred_element_type=jnp.float32)
        out_ref[chunk * group : (chunk + 1) * group, :capacity, :] = packed.reshape(
            group, capacity, LANES
        ).astype(jnp.bfloat16)
    line = lax.broadcasted_iota(jnp.int32, (8, 1), 0)
    for chunk in range(devices * 8 // CHUNK):
        pick = one_hot(in_chunk(third, chunk), CHUNK)
        packed = jnp.dot(pick, rows, preferred_element_type=jnp.float32)
        for step in range(CHUNK // 8):
            device = chunk * CHUNK // 8 + step
            block = packed[step * 8 : step * 8 + 8]
            block = jnp.where(line == 0, main_line[device : device + 1], block)
            block = jnp.where(line == 1, spare_line[device : device + 1], block)
            out_ref[device, capacity:, :] = block.astype(jnp.bfloat16)


def ordered_chunks(arrived_ref, flag_ref, count, capacity):
    devices = arrived_ref.shape[0]
    share = LANES // capacity
    lane = lax.broadcasted_iota(jnp.int32, (8, LANES), 1)
    tails = [arrived_ref[d, capacity:, :].astype(jnp.float32) for d in range(devices)]
    highs, lows, spares = [], [], []
    for first in range(0, devices, share):
        high = low = None
        for step in range(share):
            turned = step * capacity
            left = pltpu.roll(tails[first + step], turned, 1) if turned else tails[first + step]
            right = pltpu.roll(tails[first + step], (turned - capacity) % LANES, 1)
            if step:
                left = jnp.where(lane >= turned, left, high)
                right = jnp.where(lane >= turned, right, low)
            high, low = left, right
        highs.append(high[0:1])
        lows.append(low[0:1])
    for first in range(0, devices, LANES // 8):
        total = tails[first]
        for step in range(1, LANES // 8):
            total = total + tails[first + step]
        spares.append(total[1:2])
    high = jnp.concatenate(highs, axis=1)
    low = jnp.concatenate(lows, axis=1)
    spare = jnp.concatenate(spares, axis=1)
    flag_ref[0] = (jnp.max(spare) >= LOST).astype(jnp.int32)
    rows = arrived_ref[:, :capacity, :].reshape(devices * capacity, LANES)
    for chunk in range(count // CHUNK):
        pick = one_hot(jnp.where(high == chunk + 1, low, -1.0), CHUNK)
        yield jnp.dot(pick, rows, preferred_element_type=jnp.float32)
    pick = one_hot(jnp.where(high == count // CHUNK + 1, low, -1.0), WIN)
    others = jnp.concatenate(tails, axis=0).astype(jnp.bfloat16)
    yield jnp.dot(pick, rows, preferred_element_type=jnp.float32) + jnp.dot(
        one_hot(spare - 1.0, WIN), others, preferred_element_type=jnp.float32
    )


def turn_tail(rows):
    padding = jnp.zeros((LANES - rows.shape[0], LANES), jnp.float32)
    return jnp.concatenate([rows, padding], axis=0).T


def prepare_kernel(weight_ref, bias_ref, score_ref, turned_ref, floor_ref, scale_ref, base_ref):
    turned_ref[...] = weight_ref[...].astype(jnp.float32).T.astype(jnp.bfloat16)
    bias = bias_ref[...]
    score = score_ref[...].astype(jnp.float32)
    hidden = bias.shape[1]
    floor = jnp.broadcast_to(-bias, (CHUNK, hidden)).T
    floor_ref[...] = floor
    scale_ref[...] = jnp.broadcast_to(score, (CHUNK, hidden)).T
    base_ref[...] = jnp.broadcast_to(
        jnp.sum(bias * score, axis=1, keepdims=True), base_ref.shape
    )


def score_block(columns, write, turned_ref, floor_ref, scale_ref, base_ref):
    columns = columns.astype(jnp.bfloat16)
    leading = columns[:, :CHUNK]
    weight = turned_ref[...]
    for offset in range(1, WIN):
        partner = pltpu.roll(columns, columns.shape[1] - offset, 1)[:, :CHUNK]
        features = jnp.concatenate(
            [leading * partner, jnp.abs(leading - partner)], axis=0
        )
        hidden = jnp.dot(weight, features, preferred_element_type=jnp.float32)
        hidden = jnp.maximum(hidden, floor_ref[...]) * scale_ref[...]
        write(offset, jnp.sum(hidden, axis=0, keepdims=True) + base_ref[...])


def score_last(columns, limit, base, out_ref, parameters):
    place = base + lax.broadcasted_iota(jnp.int32, (1, CHUNK), 1)

    def write(offset, line):
        out_ref[offset - 1 : offset, :] = jnp.where(place + offset < limit, line, 0.0)

    score_block(columns, write, *parameters)


def main_kernel(limit_ref, arrived_ref, *refs, capacity):
    parameters = refs[:4]
    out_ref, last_ref, head_ref, flag_ref, wide_ref, scores_ref, sems = refs[4:]
    count = out_ref.shape[1]
    blocks = count // CHUNK
    for chunk, ordered in enumerate(ordered_chunks(arrived_ref, flag_ref, count, capacity)):
        if chunk < blocks:
            wide_ref[:, chunk * CHUNK : (chunk + 1) * CHUNK] = ordered.T
        else:
            wide_ref[:, count:] = turn_tail(ordered)
        if chunk == 0:
            head_ref[...] = ordered[: head_ref.shape[0]].astype(jnp.bfloat16)
    last_ref[...] = wide_ref[:, count - CHUNK : count]
    copies = []
    for block in range(blocks):
        start = block * CHUNK
        columns = wide_ref[:, start : start + CHUNK + LANES]
        place_ref = scores_ref.at[block]
        if block < blocks - 1:

            def write(offset, line, place_ref=place_ref):
                place_ref[offset - 1 : offset, :] = line

            score_block(columns, write, *parameters)
        else:
            score_last(columns, limit_ref[0], start, place_ref, parameters)
        copies.append(
            pltpu.make_async_copy(
                place_ref, out_ref.at[:, start : start + CHUNK], sems.at[block]
            )
        )
        copies[-1].start()
    for copy in copies:
        copy.wait()


def repair_kernel(limit_ref, last_ref, next_ref, *refs):
    out_ref, scores_ref, sem = refs[5:]
    base = out_ref.shape[1] - CHUNK
    following = turn_tail(next_ref[...].astype(jnp.float32))
    columns = jnp.concatenate([last_ref[...], following], axis=1)
    score_last(columns, limit_ref[0], base, scores_ref, refs[:4])
    copy = pltpu.make_async_copy(scores_ref, out_ref.at[:, base:], sem)
    copy.start()
    copy.wait()


def body(embeddings, ranks, pair_weight, pair_bias, score_weight):
    rows_dev, width = embeddings.shape
    devices = lax.axis_size("dev")
    capacity = 2 * rows_dev // devices
    hidden = pair_weight.shape[1]

    me = lax.axis_index("dev")
    outgoing = pl.pallas_call(
        functools.partial(pack_kernel, devices=devices, capacity=capacity),
        out_shape=jax.ShapeDtypeStruct((devices, capacity + 8, width), jnp.bfloat16),
        in_specs=[SMEM, ANY, ANY],
        out_specs=VMEM,
        scratch_shapes=[
            pltpu.VMEM((1, rows_dev), jnp.int32),
            pltpu.VMEM((rows_dev, width), jnp.bfloat16),
            pltpu.SemaphoreType.DMA((2,)),
        ],
        name="pack",
    )(me.astype(jnp.int32).reshape(1), ranks.reshape(1, rows_dev), embeddings)
    arrived = lax.all_to_all(outgoing, "dev", split_axis=0, concat_axis=0, tiled=True)
    parameters = pl.pallas_call(
        prepare_kernel,
        out_shape=(
            jax.ShapeDtypeStruct((hidden, 2 * width), jnp.bfloat16),
            jax.ShapeDtypeStruct((hidden, CHUNK), jnp.float32),
            jax.ShapeDtypeStruct((hidden, CHUNK), jnp.float32),
            jax.ShapeDtypeStruct((1, CHUNK), jnp.float32),
        ),
        in_specs=[VMEM] * 3,
        out_specs=(VMEM,) * 4,
        compiler_params=SMALL,
        name="prepare",
    )(pair_weight, pair_bias.reshape(1, hidden), score_weight.reshape(1, hidden))

    limit = jnp.where(me == devices - 1, rows_dev, 2 * rows_dev).astype(jnp.int32).reshape(1)
    scores, last, head, lost = pl.pallas_call(
        functools.partial(main_kernel, capacity=capacity),
        out_shape=(
            jax.ShapeDtypeStruct((WIN - 1, rows_dev), jnp.float32),
            jax.ShapeDtypeStruct((width, CHUNK), jnp.float32),
            jax.ShapeDtypeStruct((WIN, width), jnp.bfloat16),
            jax.ShapeDtypeStruct((1,), jnp.int32),
        ),
        in_specs=[SMEM] + [VMEM] * 5,
        out_specs=(HBM, VMEM, VMEM, SMEM),
        scratch_shapes=[
            pltpu.VMEM((width, rows_dev + LANES), jnp.float32),
            pltpu.VMEM((rows_dev // CHUNK, WIN - 1, CHUNK), jnp.float32),
            pltpu.SemaphoreType.DMA((rows_dev // CHUNK,)),
        ],
        compiler_params=SMALL,
        name="main",
    )(limit, arrived, *parameters)

    def repair(scores, limit, last, head, *parameters):
        following = lax.ppermute(head, "dev", [(i, i - 1) for i in range(1, devices)])
        return pl.pallas_call(
            repair_kernel,
            out_shape=jax.ShapeDtypeStruct(scores.shape, jnp.float32),
            in_specs=[SMEM] + [VMEM] * 6 + [HBM],
            out_specs=HBM,
            scratch_shapes=[
                pltpu.VMEM((WIN - 1, CHUNK), jnp.float32),
                pltpu.SemaphoreType.DMA,
            ],
            input_output_aliases={7: 0},
            compiler_params=SMALL,
            name="repair",
        )(limit, last, following, *parameters, scores)

    return lax.cond(
        lost[0] > 0,
        repair,
        lambda scores, *_: scores,
        scores, limit, last, head, *parameters,
    )


def solution(mesh):
    placed = (P("dev", None), P("dev"), P(), P(), P())
    return jax.shard_map(
        body, mesh=mesh, in_specs=placed, out_specs=P(None, "dev"), check_vma=False
    )
```

time: 36.2 us -> 36.1 us (level)
  the two profiles are of different devices: /device:TPU:1 before, /device:TPU:0 now
where the time goes in v4:
time: 36.1 us; the launch traced here: 35.8 us
  waiting for transfers between devices  16 us (44%)
  Pallas kernels  10.5 us (29%)
  starting transfers between devices  7.33 us (20%)
  local copies, waits for them, and re-layouts  1.3 us (4%)
  between operations  0.72 us (2%)
    all_to_all x1, waiting for transfers between devices, body(): lax.all_to_all(outgoing, 'dev', split_axis=0, concat_axis=0, tiled=True)  16 us
    all_to_all x1, starting transfers between devices, body(): lax.all_to_all(outgoing, 'dev', split_axis=0, concat_axis=0, tiled=True)  7.33 us
    pallas_call x1, Pallas kernels, body(): pl.pallas_call(functools.partial(main_kernel, capacity=capacity), out_sha...  6.67 us
    pallas_call x1, Pallas kernels, body(): pl.pallas_call(functools.partial(pack_kernel, devices=devices, capacity=c...  3.69 us
    unnamed x8, local copies, waits for them, and re-layouts  1.3 us
  transfers between devices with their start and end apart: 1, of which 1 were waited for; matrix products, arithmetic and copies ran while one was open for 0% of the time, Pallas kernels for 0%

profile of v4, /device:TPU:0, one launch (start us, length us, event | category | flops | bytes accessed | tf_op | source)
XLA Modules:
  0.0 35.8 jit_solution(1159206096923631325)
XLA Ops:
  0.0 3.7 %pack.1 = bf16[32,72,128]{2,1,0:T(8,128)(2,1)} custom-call(s32[1]{0:T(128)} %bitcast.1.me_ref, s32[1,1024]{1,0:T(1,128)} %bitcast.8, bf16[1024,128]{1,0:T(8,128)(2,1)} %rows_hbm.1), custom_call_target="tpu_custom_call" | custom-call | tf_op jit(solution)/shard_map/pack/pallas_call | solution.py:297
  3.7 0.0 copy-start
  3.7 7.3 %all-to-all-start = ((bf16[32,72,128]{2,1,0:T(8,128)(2,1)}), bf16[32,72,128]{2,1,0:T(8,128)(2,1)S(1)}, u32[]{:S(2)}, u32[]{:S(2)}) async-start(bf16[32,72,128]{2,1,0:T(8,128)(2,1)} %pack.1), calls=%async_computation | async-start | bytes 1179648 | tf_op jit(solution)/shard_map/all_to_all | solution.py:309
  11.1 0.0 copy-start.1
  11.1 0.0 copy-start.2
  11.1 0.0 copy-done
  11.1 0.6 %copy-done.1 = f32[128]{0:T(128)S(1)} copy-done((f32[128]{0:T(128)S(1)}, f32[128]{0:T(128)}, u32[]{:S(2)}) %copy-start.1) | copy-done | bytes 536
  11.7 0.0 copy-done.2
  11.7 0.1 prepare.1
  11.9 16.0 %all-to-all-done.arrived_ref = bf16[32,72,128]{2,1,0:T(8,128)(2,1)S(1)} async-done(((bf16[32,72,128]{2,1,0:T(8,128)(2,1)}), bf16[32,72,128]{2,1,0:T(8,128)(2,1)S(1)}, u32[]{:S(2)}, u32[]{:S(2)}) %all-to-all-start) | async-done | bytes 589856 | tf_op jit(solution)/shard_map/all_to_all | solution.py:309
  27.9 6.7 %main.1 = (f32[31,1024]{1,0:T(8,128)S(1)}, f32[128,256]{1,0:T(8,128)S(1)}, bf16[32,128]{1,0:T(8,128)(2,1)S(1)}, s32[1]{0:T(128)}) custom-call(s32[1]{0:T(128)} %bitcast.limit_ref, bf16[32,72,128]{2,1,0:T(8,128)(2,1)S(1)} %all-to-all-done.arrived_ref, bf16[128,256]{1,0:T(8,128)(2,1)S(1)} %get-tuple-element.41.refs_0_, ...), custom_call_target="tpu_custom_call" | custom-call | tf_op jit(solution)/shard_map/main/pallas_call | solution.py:325
  35.2 0.0 copy-start.3
  35.2 0.6 %copy-done.3 = f32[31,1024]{1,0:T(8,128)} copy-done((f32[31,1024]{1,0:T(8,128)}, f32[31,1024]{1,0:T(8,128)S(1)}, u32[]{:S(2)}) %copy-start.3) | copy-done | bytes 127000
  (1 shorter events, 0.0 us)
Async XLA Ops:
  3.7 7.4 %copy-start = (bf16[256,128]{1,0:T(8,128)(2,1)S(1)}, bf16[256,128]{1,0:T(8,128)(2,1)}, u32[]{:S(2)}) copy-start(bf16[256,128]{1,0:T(8,128)(2,1)} %weight_ref.1) | copy-start | bytes 196612
  3.7 24.1 %all-to-all-start = ((bf16[32,72,128]{2,1,0:T(8,128)(2,1)}), bf16[32,72,128]{2,1,0:T(8,128)(2,1)S(1)}, u32[]{:S(2)}, u32[]{:S(2)}) async-start(bf16[32,72,128]{2,1,0:T(8,128)(2,1)} %pack.1), calls=%async_computation | async-start | bytes 1179648 | tf_op jit(solution)/shard_map/all_to_all | solution.py:309
  11.1 0.7 %copy-start.1 = (f32[128]{0:T(128)S(1)}, f32[128]{0:T(128)}, u32[]{:S(2)}) copy-start(f32[128]{0:T(128)} %param.10) | copy-start | bytes 1540
  11.1 0.7 %copy-start.2 = (bf16[128]{0:T(256)(128)(2,1)S(1)}, bf16[128]{0:T(256)(128)(2,1)}, u32[]{:S(2)}) copy-start(bf16[128]{0:T(256)(128)(2,1)} %param.11) | copy-start | bytes 772
  35.2 0.7 %copy-start.3 = (f32[31,1024]{1,0:T(8,128)}, f32[31,1024]{1,0:T(8,128)S(1)}, u32[]{:S(2)}) copy-start(f32[31,1024]{1,0:T(8,128)S(1)} %get-tuple-element.56) | copy-start | bytes 380932
